TPU v7x, 32 devices: a whole 2x2x4 slice. The times are simulated.
32 devices in a mesh: group: 2 (over x), date: 16 (over z, y, core).
Axes of the slice: x: 2, y: 2, z: 4, core: 2. Of those that a mesh axis runs over, the one named last changes fastest.
Arguments:
- salvo_records: bfloat16 [32, 3, 2, 13, 1024], P(('group', 'date')), parts along dimension 0, may hold values from -6 to 6
- stencil_weights: bfloat16 [32, 3, 8], P(('group', 'date')), parts along dimension 0, may hold values from -2 to 2
- zone_drifts: int32 [32, 3], P(('group', 'date')), parts along dimension 0, may hold values from -16 to 16
- seam_sweeps: int32 [32, 2], P(('group', 'date')), parts along dimension 0, may hold values from 1 to 2
- prior_sweeps: int32 [32], P(('group', 'date')), parts along dimension 0, may hold values from 0 to 1
- viewing_frames: int32 [512, 128], P(('group', 'date')), parts along dimension 0, may hold values from 0 to 4095, as said below
Outputs:
- filtered: bfloat16 [32, 2, 32, 1024], P(('group', 'date')), parts along dimension 0
There are 2 independent parts, one for each index of `group`. A program takes and returns all parts, laid end to end along the dimension named above; each array names one. Nothing has to cross between parts.
Inputs may be any that keep to these rules, and one draw needn't show every extreme that they name: `viewing_frames`: window w belongs to ground block g = w // 16 and names pixels line-major among 4 lines of 1024 cells: local line 0 is the line above the block, lines 1 .. 2 the block, line 3 the line below. The first block never names local line 0, the last block never names local line 3.
All inputs are finite; a program needn't handle non-finite values.
Results may differ from a plain program's by a relative error of at most 0.019.
Values may be sent and summed in bfloat16 or wider, within the bound.
No kernel may reach another device: no remote copies, remote signals or barrier semaphores. Data moves between devices by JAX's collectives and lax.ppermute only.
A program may use at most 64 MiB of HBM per device.

v0:
```python
import math

import jax
import jax.numpy as jnp
from jax import lax
from jax.sharding import PartitionSpec as P

LB = 2
SALVO_TALLY = 3
STENCIL_WEIGHTS = 8
LOOKS = 128
ITERS = 8
PATCH = 32


EPSILON = 1e-06
SHRINK = 0.05


def padded(block, sides, width):
    for axis, dim in sides:
        count = lax.axis_size(axis)
        forward = [(i, i + 1) for i in range(count - 1)]
        backward = [(target, source) for source, target in forward]
        low = lax.ppermute(
            lax.slice_in_dim(block, block.shape[dim] - width, None, axis=dim), axis, forward
        )
        high = lax.ppermute(lax.slice_in_dim(block, 0, width, axis=dim), axis, backward)
        block = jnp.concatenate([low, block, high], axis=dim)
    return block


def regridding_tableau(tap_row, offset, distance_readings):
    rows = lax.broadcasted_iota(jnp.int32, (distance_readings, distance_readings), 0)
    downward_entry_list = lax.broadcasted_iota(jnp.int32, (distance_readings, distance_readings), 1)
    distance = rows - downward_entry_list - offset + (STENCIL_WEIGHTS // 2 - 1)
    matrix = jnp.zeros((distance_readings, distance_readings), jnp.bfloat16)
    for tap_index in range(STENCIL_WEIGHTS):
        matrix = jnp.where(distance == tap_index, tap_row[tap_index], matrix)
    return matrix


def seam_lone_capture(
    piled_salvos, stencil_weight_table, distance_drifts, joint_sweep, opening_salvo, sweep_labels
):
    distance_readings = piled_salvos.shape[-1]
    sweeps_each_salvo = piled_salvos.shape[2]
    regridding_zones = jnp.stack(
        [
            regridding_tableau(
                stencil_weight_table[salvo_label], distance_drifts[salvo_label], distance_readings
            )
            for salvo_label in range(SALVO_TALLY)
        ]
    )
    regridded_salvos = jnp.einsum(
        "bndo,bot->bndt", piled_salvos, regridding_zones, preferred_element_type=jnp.float32
    ).astype(jnp.bfloat16)
    sweep_spacing = sweeps_each_salvo - joint_sweep
    salvo_beginnings = (
        jnp.concatenate([jnp.zeros((1,), jnp.int32), jnp.cumsum(sweep_spacing)]) - opening_salvo
    )
    flight_sweep_slot = lax.broadcasted_iota(jnp.int32, (sweep_labels, sweeps_each_salvo), 0)
    sweep_slot = lax.broadcasted_iota(jnp.int32, (sweep_labels, sweeps_each_salvo), 1)
    downward_entry_list = []
    for salvo_label in range(SALVO_TALLY):
        seam_ramp = jnp.ones((sweep_labels, sweeps_each_salvo), jnp.float32)
        if salvo_label > 0:
            upward_ramp = (flight_sweep_slot - salvo_beginnings[salvo_label] + 1).astype(
                jnp.float32
            ) / (joint_sweep[salvo_label - 1] + 1).astype(jnp.float32)
            seam_ramp = seam_ramp * jnp.clip(upward_ramp, 0.0, 1.0)
        if salvo_label < SALVO_TALLY - 1:
            downward_ramp = (
                salvo_beginnings[salvo_label] + sweeps_each_salvo - flight_sweep_slot
            ).astype(jnp.float32) / (joint_sweep[salvo_label] + 1).astype(jnp.float32)
            seam_ramp = seam_ramp * jnp.clip(downward_ramp, 0.0, 1.0)
        downward_entry_list.append(
            jnp.where(
                flight_sweep_slot == salvo_beginnings[salvo_label] + sweep_slot, seam_ramp, 0.0
            ).astype(jnp.bfloat16)
        )
    sweep_target_slot = jnp.stack(downward_entry_list, axis=1)
    return jnp.einsum(
        "tzg,zugi->uti", sweep_target_slot, regridded_salvos, preferred_element_type=jnp.float32
    ).astype(jnp.bfloat16)


def coupling_frames(readings, native_picture_elements):
    sample_real = readings[:, 0]
    sample_imaginary = readings[:, 1]

    def pair(left, right):
        return jnp.einsum("dwm,ewm->wde", left, right, preferred_element_type=jnp.float32)

    inverse_looks = 1.0 / LOOKS
    covariance_real = (
        pair(sample_real, sample_real) + pair(sample_imaginary, sample_imaginary)
    ) * inverse_looks
    mixed = pair(sample_imaginary, sample_real)
    covariance_imaginary = (mixed - jnp.swapaxes(mixed, 1, 2)) * inverse_looks
    dates = readings.shape[0]
    inverse_root = lax.rsqrt(jnp.diagonal(covariance_real, axis1=1, axis2=2) + EPSILON)
    outer = inverse_root[:, :, None] * inverse_root[:, None, :]
    identity = jnp.eye(dates, dtype=jnp.float32)
    coherence_real = (1.0 - SHRINK) * covariance_real * outer + SHRINK * identity
    coherence_imaginary = (1.0 - SHRINK) * covariance_imaginary * outer
    vector_real = jnp.ones(inverse_root.shape, jnp.float32)
    vector_imaginary = jnp.zeros(inverse_root.shape, jnp.float32)

    def apply_matrix(matrix, vector):
        return jnp.einsum("wde,we->wd", matrix, vector, precision=lax.Precision.HIGHEST)

    for iteration in range(ITERS):
        image_real = apply_matrix(coherence_real, vector_real) - apply_matrix(
            coherence_imaginary, vector_imaginary
        )
        image_imaginary = apply_matrix(coherence_real, vector_imaginary) + apply_matrix(
            coherence_imaginary, vector_real
        )
        factor = lax.rsqrt(
            jnp.mean(
                image_real * image_real + image_imaginary * image_imaginary, axis=1, keepdims=True
            )
            + EPSILON
        )
        vector_real = image_real * factor
        vector_imaginary = image_imaginary * factor
    coupled_result = jnp.stack([vector_real, vector_imaginary]).astype(jnp.bfloat16)

    def project(history, pixels):
        return jnp.einsum("wd,dwm->wm", history, pixels, preferred_element_type=jnp.float32)

    scaling = 1.0 / math.sqrt(dates)
    own_real = native_picture_elements[:, 0]
    own_imaginary = native_picture_elements[:, 1]
    compressed_real = (
        project(coupled_result[0], own_real) + project(coupled_result[1], own_imaginary)
    ) * scaling
    compressed_imaginary = (
        project(coupled_result[0], own_imaginary) - project(coupled_result[1], own_real)
    ) * scaling
    condensed_result = jnp.stack([compressed_real, compressed_imaginary]).astype(jnp.bfloat16)
    return (condensed_result, coupled_result)


def dft_tables(length, span):
    first = lax.broadcasted_iota(jnp.int32, (span, span), 0)
    second = lax.broadcasted_iota(jnp.int32, (span, span), 1)
    product = first % length * (second % length) % length
    angle = product.astype(jnp.float32) * (2.0 * math.pi / length)
    inside = first // length == second // length
    cosine = jnp.where(inside, jnp.cos(angle), 0.0).astype(jnp.bfloat16)
    sine = jnp.where(inside, jnp.sin(angle), 0.0).astype(jnp.bfloat16)
    return (cosine, sine)


def goldstein(rebuilt):
    sweep_labels = rebuilt.shape[1]
    distance_readings = rebuilt.shape[2]
    range_cos, range_sin = dft_tables(PATCH, 128)
    line_cos, line_sin = dft_tables(PATCH, PATCH)

    def across(matrix, table):
        return jnp.dot(matrix.reshape(-1, 128), table, preferred_element_type=jnp.float32).reshape(
            sweep_labels, distance_readings
        )

    def along(table, matrix):
        return jnp.einsum(
            "kn,pnr->pkr",
            table,
            matrix.reshape(sweep_labels // PATCH, PATCH, distance_readings),
            preferred_element_type=jnp.float32,
        )

    real_in = rebuilt[0]
    imaginary_in = rebuilt[1]
    first_real = (across(real_in, range_cos) + across(imaginary_in, range_sin)).astype(jnp.bfloat16)
    first_imaginary = (across(imaginary_in, range_cos) - across(real_in, range_sin)).astype(
        jnp.bfloat16
    )
    spectrum_real = along(line_cos, first_real) + along(line_sin, first_imaginary)
    spectrum_imaginary = along(line_cos, first_imaginary) - along(line_sin, first_real)
    power = spectrum_real * spectrum_real + spectrum_imaginary * spectrum_imaginary
    patch_total = (
        jnp.sum(power, axis=1)
        .reshape(sweep_labels // PATCH, distance_readings // PATCH, PATCH)
        .sum(axis=2)
    )
    patch_mean = jnp.repeat(patch_total / (PATCH * PATCH), PATCH, axis=1)[:, None, :]
    seam_ramp = jnp.sqrt(jnp.sqrt(power / (patch_mean + EPSILON)))
    weighted_real = (spectrum_real * seam_ramp).astype(jnp.bfloat16)
    weighted_imaginary = (spectrum_imaginary * seam_ramp).astype(jnp.bfloat16)
    back_real = (along(line_cos, weighted_real) - along(line_sin, weighted_imaginary)).astype(
        jnp.bfloat16
    )
    back_imaginary = (along(line_cos, weighted_imaginary) + along(line_sin, weighted_real)).astype(
        jnp.bfloat16
    )
    scaling = 1.0 / (PATCH * PATCH)
    out_real = (
        (across(back_real, range_cos) - across(back_imaginary, range_sin)) * scaling
    ).astype(jnp.bfloat16)
    out_imaginary = (
        (across(back_imaginary, range_cos) + across(back_real, range_sin)) * scaling
    ).astype(jnp.bfloat16)
    return jnp.stack([out_real, out_imaginary])


def on_device(
    salvo_records, stencil_weights, zone_drifts, seam_sweeps, prior_sweeps, viewing_frames
):
    devices = lax.axis_size("date")
    sweep_labels = LB * devices
    seamed_picture = seam_lone_capture(
        salvo_records[0],
        stencil_weights[0],
        zone_drifts[0],
        seam_sweeps[0],
        prior_sweeps[0],
        sweep_labels,
    )
    distance_readings = seamed_picture.shape[2]
    ground = lax.all_to_all(seamed_picture[None], "date", split_axis=2, concat_axis=0, tiled=True)
    extended = padded(ground, (("date", 2),), 1)
    windows_here = viewing_frames.shape[0]
    flat = extended.reshape(devices, 2, (LB + 2) * distance_readings)
    readings = jnp.take(flat, viewing_frames.reshape(-1), axis=2).reshape(
        devices, 2, windows_here, LOOKS
    )
    native_picture_elements = extended[:, :, 1 : LB + 1].reshape(devices, 2, windows_here, LOOKS)
    condensed_result, coupled_result = coupling_frames(readings, native_picture_elements)
    history_real = coupled_result[0].astype(jnp.float32).T[:, :, None]
    history_imaginary = coupled_result[1].astype(jnp.float32).T[:, :, None]
    value_real = condensed_result[0].astype(jnp.float32)[None]
    value_imaginary = condensed_result[1].astype(jnp.float32)[None]
    rebuilt = jnp.stack(
        [
            value_real * history_real - value_imaginary * history_imaginary,
            value_real * history_imaginary + value_imaginary * history_real,
        ],
        axis=1,
    ).astype(jnp.bfloat16)
    rebuilt = rebuilt.reshape(devices, 2, LB, distance_readings)
    mine = lax.all_to_all(rebuilt, "date", split_axis=0, concat_axis=2, tiled=True)[0]
    return goldstein(mine)[None]


def solution(mesh):
    in_specs = (
        P(("group", "date"), None, None, None, None),
        P(("group", "date"), None, None),
        P(("group", "date"), None),
        P(("group", "date"), None),
        P(("group", "date")),
        P(("group", "date"), None),
    )
    out_specs = P(("group", "date"), None, None, None)
    return jax.shard_map(
        on_device, mesh=mesh, in_specs=in_specs, out_specs=out_specs, check_vma=False
    )
```

profile of v0, /device:TPU:0, one launch (start us, length us, event | category | flops | bytes accessed | tf_op | source)
XLA Modules:
  0.0 115.1 jit_solution(11993288917228165708)
XLA Ops:
  0.0 2.1 %fusion.145 = (bf16[1,1,1]{2,1,0:T(2,128)(2,1)}, bf16[1,1,1]{2,1,0:T(2,128)(2,1)}, bf16[1,1,1]{2,1,0:T(2,128)(2,1)}, bf16[1,1,1]{2,1,0:T(2,128)(2,1)}, bf16[1,1,...) fusion(bf16[1,3,8]{2,1,0:T(4,128)(2,1)} %param.7), kind=kLoop, calls=%fused_computation.249 | loop fusion | bytes 76 | tf_op jit(solution)/shard_map/slice | solution.py:39
  2.1 1.5 %fusion.146 = (bf16[1,1,1]{2,1,0:T(2,128)(2,1)}, bf16[1,1,1]{2,1,0:T(2,128)(2,1)}, bf16[1,1,1]{2,1,0:T(2,128)(2,1)}, bf16[1,1,1]{2,1,0:T(2,128)(2,1)}, bf16[1,1,1]{2,1,0:T(2,128)(2,1)}) fusion(bf16[1,3,8]{2,1,0:T(4,128)(2,1)} %param.7), kind=kLoop, calls=%fused_computation.250 | loop fusion | bytes 20 | tf_op jit(solution)/shard_map/slice | solution.py:39
  3.6 0.7 subtract_bitcast_fusion
  4.3 1.4 %fusion.148 = (s32[1,1]{1,0:T(1,128)}, s32[1,1]{1,0:T(1,128)}) fusion(s32[1,2]{1,0:T(1,128)} %param.9), kind=kLoop, calls=%fused_computation.252 | loop fusion | bytes 16 | tf_op jit(solution)/shard_map/slice | solution.py:76
  6.6 0.7 fusion.147
  7.2 0.6 iota_add_fusion.1
  9.0 0.7 iota_add_fusion.2
  9.7 1.4 %fusion.149 = (s32[1,1]{1,0:T(1,128)}, s32[1,1]{1,0:T(1,128)}, s32[1,1]{1,0:T(1,128)}) fusion(s32[1,3]{1,0:T(1,128)} %param.8), kind=kLoop, calls=%fused_computation.253 | loop fusion | bytes 24 | tf_op jit(solution)/shard_map/slice | solution.py:51
  12.3 0.7 iota_add_fusion
  13.0 1.2 %divide_clamp_fusion = (bf16[32]{0:T(256)(128)(2,1)S(1)}, bf16[32]{0:T(256)(128)(2,1)S(1)}) fusion(s32[]{:T(128)} %bitcast.37, f32[]{:T(128)} %bitcast.36, s32[]{:T(128)S(6)} %add.411, f32[]{:T(128)} %bitcast.34, s32[]{:T(128)} %bitcast.35), kind=kLoop, calls=%fused_computation.209 | loop fusion | flops 544 | bytes 148 | tf_op jit(solution)/shard_map/jit(clip)/min | solution.py:72
  14.5 9.4 %fusion.41 = bf16[1,1024,1024]{2,1,0:T(8,128)(2,1)} fusion(s32[]{:T(128)} %bitcast, bf16[]{:T(256)} %bitcast.8, bf16[]{:T(256)} %bitcast.7, bf16[]{:T(256)} %bitcast.6, bf16[]{:T(256)} %bitcast.5, bf16[]{:T(256)} %bitcast.4, bf16[]{:T(256)} %bitcast.3, bf16[]{:T(256)} %bitcast.2, bf16[]{:T(256)} %bitcast.1), kind=kLoop, calls=%fused_computation.48 | loop fusion | flops 19922944 | bytes 2097172 | tf_op jit(solution)/shard_map/jit(_where)/select_n | solution.py:39
  23.9 17.7 %fusion.25 = (bf16[1,1024,1024]{2,1,0:T(8,128)(2,1)S(1)}, bf16[1,1024,1024]{2,1,0:T(8,128)(2,1)}) fusion(s32[]{:T(128)} %bitcast.18, bf16[]{:T(256)} %bitcast.26, bf16[]{:T(256)} %bitcast.25, bf16[]{:T(256)} %bitcast.24, bf16[]{:T(256)} %bitcast.23, bf16[]{:T(256)} %bitcast.22, bf16[]{:T(256)} %bitcast.21, bf16[]{:T(256)} %bitcast.20, bf16[]{:T(256)} %bitcast.19, ...), kind=kLoop, calls=%fused_computation.32 | loop fusion | flops 38797312 | bytes 4194344 | tf_op jit(solution)/shard_map/jit(_where)/select_n | solution.py:39
  41.6 3.5 %fusion.52 = bf16[1,2,32,1024]{3,2,1,0:T(8,128)(2,1)S(1)} fusion(bf16[1,1024,1024]{2,1,0:T(8,128)(2,1)S(1)} %get-tuple-element.99, bf16[1,1024,1024]{2,1,0:T(8,128)(2,1)} %get-tuple-element.100, bf16[1,1024,1024]{2,1,0:T(8,128)(2,1)} %fusion.41, bf16[3,2,13,1024]{3,1,2,0:T(2,128)(2,1)S(1)} %bitcast.325, bf16[32,1,13]{0,2,1:T(8,128)(2,1)S(1)} %select_convert_fusion.4, ...), kind=kOutput, calls=%fused_computation.61 | convolution fusion | flops 187711936 | bytes 6584768 | tf_op jit(solution)/shard_map/tzg,zugi->uti/dot_general | solution.py:84
  45.1 0.8 copy.59
  45.9 7.4 %all-to-all-start = ((bf16[1,2,32,1024]{3,1,0,2:T(2,128)(2,1)}), bf16[1,2,32,1024]{3,1,0,2:T(2,128)(2,1)S(1)}, u32[]{:S(2)}, u32[]{:S(2)}) async-start(bf16[1,2,32,1024]{3,1,0,2:T(2,128)(2,1)} %copy.59), calls=%async_computation | async-start | bytes 262144 | tf_op jit(solution)/shard_map/all_to_all | solution.py:225
  53.4 7.8 %all-to-all-done = bf16[1,2,32,1024]{3,1,0,2:T(2,128)(2,1)S(1)} async-done(((bf16[1,2,32,1024]{3,1,0,2:T(2,128)(2,1)}), bf16[1,2,32,1024]{3,1,0,2:T(2,128)(2,1)S(1)}, u32[]{:S(2)}, u32[]{:S(2)}) %all-to-all-start) | async-done | bytes 131104 | tf_op jit(solution)/shard_map/all_to_all | solution.py:225
  61.3 1.3 %collective-permute-start = (bf16[16,2,1,1024]{3,0,2,1:T(8,128)(2,1)S(1)}, bf16[16,2,1,1024]{3,0,2,1:T(8,128)(2,1)S(1)}, u32[]{:S(2)}, u32[]{:S(2)}) collective-permute-start(bf16[16,2,1,1024]{3,0,2,1:T(8,128)(2,1)S(1)} %get-tuple-element.39), channel_id=1, source_target_pairs={{0,1},{1,2},{2,3},{3,4},{4,5},{5,6},{6,7},{7,8},{8,9},{9,10},{10,1... | collective-permute-start | bytes 196616 | tf_op jit(solution)/shard_map/ppermute | solution.py:25
  62.6 1.5 %collective-permute-start.1 = (bf16[16,2,1,1024]{3,0,2,1:T(8,128)(2,1)S(1)}, bf16[16,2,1,1024]{3,0,2,1:T(8,128)(2,1)S(1)}, u32[]{:S(2)}, u32[]{:S(2)}) collective-permute-start(bf16[16,2,1,1024]{3,0,2,1:T(8,128)(2,1)S(1)} %get-tuple-element.40), channel_id=1, source_target_pairs={{1,0},{2,1},{3,2},{4,3},{5,4},{6,5},{7,6},{8,7},{9,8},{10,9},{11,1... | collective-permute-start | bytes 196616 | tf_op jit(solution)/shard_map/ppermute | solution.py:28
  64.3 1.4 %collective-permute-done.1 = bf16[16,2,1,1024]{3,0,2,1:T(8,128)(2,1)S(1)} collective-permute-done((bf16[16,2,1,1024]{3,0,2,1:T(8,128)(2,1)S(1)}, bf16[16,2,1,1024]{3,0,2,1:T(8,128)(2,1)S(1)}, u32[]{:S(2)}, u32[]{:S(2)}) %collective-permute-start.1) | collective-permute-done | bytes 65568 | tf_op jit(solution)/shard_map/ppermute | solution.py:28
  65.8 1.5 %copy.61 = bf16[16,2,4,1024]{0,1,3,2:T(2,128)(2,1)S(1)} copy(bf16[16,2,4,1024]{3,0,2,1:T(8,128)(2,1)S(1)} %pad_maximum_fusion) | data formatting | bytes 524288 | tf_op jit(solution)/shard_map/concatenate | solution.py:29
  67.2 7.1 %gather_fusion = bf16[2048,16,2]{1,2,0:T(2,128)(2,1)S(1)} fusion(bf16[16,2,4096]{0,1,2:T(2,128)(2,1)S(1)} %bitcast.326, s32[2048]{0:T(1024)S(1)} %broadcast_clamp_fusion), kind=kCustom, calls=%fused_computation | custom fusion | bytes 270336 | tf_op jit(solution)/shard_map/jit(_take)/gather | solution.py:229
  74.3 0.7 copy.63
  75.6 0.6 gather_fusion.1
  77.6 0.4 fusion.139
  78.2 0.4 fusion.137
  79.3 0.4 fusion.135
  79.9 0.4 fusion.133
  81.0 0.4 fusion.131
  81.7 0.4 fusion.129
  82.7 0.4 fusion.127
  83.4 0.4 fusion.125
  84.4 0.4 fusion.123
  85.1 0.4 fusion.121
  86.1 0.4 fusion.119
  86.8 0.4 fusion.117
  88.5 0.4 fusion.113
  91.5 0.8 pad_maximum_fusion.1
  92.3 7.2 %all-to-all-start.1 = ((bf16[16,2,2,1024]{3,2,1,0:T(2,128)(2,1)}), bf16[16,2,2,1024]{3,2,1,0:T(2,128)(2,1)S(1)}, u32[]{:S(2)}, u32[]{:S(2)}) async-start(bf16[16,2,2,1024]{3,2,1,0:T(2,128)(2,1)} %pad_maximum_fusion.1), calls=%async_computation.1 | async-start | bytes 262144 | tf_op jit(solution)/shard_map/all_to_all | solution.py:246
  99.5 7.9 %all-to-all-done.1 = bf16[16,2,2,1024]{3,2,1,0:T(2,128)(2,1)S(1)} async-done(((bf16[16,2,2,1024]{3,2,1,0:T(2,128)(2,1)}), bf16[16,2,2,1024]{3,2,1,0:T(2,128)(2,1)S(1)}, u32[]{:S(2)}, u32[]{:S(2)}) %all-to-all-start.1) | async-done | bytes 131104 | tf_op jit(solution)/shard_map/all_to_all | solution.py:246
  107.6 0.5 fusion.105
  108.1 0.5 fusion.106
  108.6 0.5 fusion.60
  109.1 0.5 fusion.59
  112.1 0.5 fusion.104
  112.9 0.5 fusion.103
  113.4 0.5 fusion.57
  113.9 0.5 fusion.58
  114.5 0.7 maximum_bitcast_fusion.10
  (120 shorter events, 14.1 us)
Async XLA Ops:
  0.0 41.6 %copy-start = (bf16[1,3,2,13,1024]{4,2,3,1,0:T(2,128)(2,1)S(1)}, bf16[1,3,2,13,1024]{4,2,3,1,0:T(2,128)(2,1)}, u32[]{:S(2)}) copy-start(bf16[1,3,2,13,1024]{4,2,3,1,0:T(2,128)(2,1)} %param.6) | copy-start | bytes 479236
  41.6 11.8 %copy-start.1 = (s32[16,128]{1,0:T(8,128)S(1)}, s32[16,128]{1,0:T(8,128)}, u32[]{:S(2)}) copy-start(s32[16,128]{1,0:T(8,128)} %param.11) | copy-start | bytes 24580
  45.9 15.3 %all-to-all-start = ((bf16[1,2,32,1024]{3,1,0,2:T(2,128)(2,1)}), bf16[1,2,32,1024]{3,1,0,2:T(2,128)(2,1)S(1)}, u32[]{:S(2)}, u32[]{:S(2)}) async-start(bf16[1,2,32,1024]{3,1,0,2:T(2,128)(2,1)} %copy.59), calls=%async_computation | async-start | bytes 262144 | tf_op jit(solution)/shard_map/all_to_all | solution.py:225
  61.3 3.0 %collective-permute-start = (bf16[16,2,1,1024]{3,0,2,1:T(8,128)(2,1)S(1)}, bf16[16,2,1,1024]{3,0,2,1:T(8,128)(2,1)S(1)}, u32[]{:S(2)}, u32[]{:S(2)}) collective-permute-start(bf16[16,2,1,1024]{3,0,2,1:T(8,128)(2,1)S(1)} %get-tuple-element.39), channel_id=1, source_target_pairs={{0,1},{1,2},{2,3},{3,4},{4,5},{5,6},{6,7},{7,8},{8,9},{9,10},{10,1... | collective-permute-start | bytes 196616 | tf_op jit(solution)/shard_map/ppermute | solution.py:25
  62.6 3.1 %collective-permute-start.1 = (bf16[16,2,1,1024]{3,0,2,1:T(8,128)(2,1)S(1)}, bf16[16,2,1,1024]{3,0,2,1:T(8,128)(2,1)S(1)}, u32[]{:S(2)}, u32[]{:S(2)}) collective-permute-start(bf16[16,2,1,1024]{3,0,2,1:T(8,128)(2,1)S(1)} %get-tuple-element.40), channel_id=1, source_target_pairs={{1,0},{2,1},{3,2},{4,3},{5,4},{6,5},{7,6},{8,7},{9,8},{10,9},{11,1... | collective-permute-start | bytes 196616 | tf_op jit(solution)/shard_map/ppermute | solution.py:28
  92.3 15.1 %all-to-all-start.1 = ((bf16[16,2,2,1024]{3,2,1,0:T(2,128)(2,1)}), bf16[16,2,2,1024]{3,2,1,0:T(2,128)(2,1)S(1)}, u32[]{:S(2)}, u32[]{:S(2)}) async-start(bf16[16,2,2,1024]{3,2,1,0:T(2,128)(2,1)} %pad_maximum_fusion.1), calls=%async_computation.1 | async-start | bytes 262144 | tf_op jit(solution)/shard_map/all_to_all | solution.py:246
where the time goes:
time: 116 us; the launch traced here: 115 us
  other arithmetic  35.1 us (30%)
  matrix products  22.4 us (19%)
  local copies, waits for them, and re-layouts  19.4 us (17%)
  starting transfers between devices  17.4 us (15%)
  waiting for transfers between devices  17 us (15%)
  between operations  3.85 us (3%)
    select_n x2, other arithmetic, regridding_tableau(): matrix = jnp.where(distance == tap_index, tap_row[tap_index], matrix)  27.1 us
    dot_general x32, matrix products, apply_matrix(): jnp.einsum('wde,we->wd', matrix, vector, precision=lax.Precision.HIGHEST)  11.8 us
    all_to_all x1, waiting for transfers between devices, on_device(): lax.all_to_all(rebuilt, 'date', split_axis=0, concat_axis=2, tiled=True)[0]  7.86 us
    all_to_all x1, waiting for transfers between devices, on_device(): lax.all_to_all(seamed_picture[None], 'date', split_axis=2, concat_axis=0,...  7.78 us
    gather x2, local copies, waits for them, and re-layouts, on_device(): jnp.take(flat, viewing_frames.reshape(-1), axis=2)  7.75 us
    all_to_all x1, starting transfers between devices, on_device(): lax.all_to_all(seamed_picture[None], 'date', split_axis=2, concat_axis=0,...  7.41 us
    all_to_all x1, starting transfers between devices, on_device(): lax.all_to_all(rebuilt, 'date', split_axis=0, concat_axis=2, tiled=True)[0]  7.21 us
    dot_general x8, matrix products, across(): jnp.dot(matrix.reshape(-1, 128), table, preferred_element_type=jnp.float32)  3.82 us
  transfers between devices with their start and end apart: 4, of which 3 were waited for; matrix products, arithmetic and copies ran while one was open for 0% of the time, Pallas kernels for 0%

commit v1 on v0

v1 whole, which is shorter than its diff:
```python
import functools
import math

import jax
import jax.numpy as jnp
import numpy as np
from jax import lax
from jax.experimental import pallas as pl
from jax.experimental.pallas import tpu as pltpu
from jax.sharding import PartitionSpec as P

LB = 2
SALVO_TALLY = 3
STENCIL_WEIGHTS = 8
LOOKS = 128
ITERS = 8
PATCH = 32
LANES = 128

EPSILON = 1e-06
SHRINK = 0.05

HALO = LB + 2
F32 = jnp.float32
BF16 = jnp.bfloat16
NT = (((1,), (1,)), ((), ()))


def iota(shape, axis):
    return lax.broadcasted_iota(jnp.int32, shape, axis)


def seam_kernel(drifts, seams, prior, weights, bursts, out, held, *, sweep_labels):
    sweeps, cells = bursts.shape[3:]
    slot = held.shape[0] // (2 * SALVO_TALLY)
    span = cells + LANES
    held[...] = jnp.zeros(held.shape, held.dtype)
    taps = weights[0].astype(F32)
    for b in range(SALVO_TALLY):
        first = span + (STENCIL_WEIGHTS // 2 - 1) - drifts[0, b]
        first = jnp.where(first >= span, first - span, first)
        for c in range(2):
            row = jnp.concatenate(
                [bursts[0, b, c].astype(F32), jnp.zeros((sweeps, LANES), F32)], axis=1
            )
            row = pltpu.roll(row, first, 1)
            total = row * taps[b : b + 1, 0:1]
            for k in range(1, STENCIL_WEIGHTS):
                total = total + pltpu.roll(row, span - k, 1) * taps[b : b + 1, k : k + 1]
            base = (c * SALVO_TALLY + b) * slot
            held[base : base + sweeps, :] = total[:, :cells].astype(BF16)
    shape = (out.shape[0] * 2 * HALO, held.shape[0])
    bits = slot.bit_length() - 1
    row, column = iota(shape, 0), iota(shape, 1)
    line = (row // (2 * HALO)) * LB - 1 + row % HALO
    part = (row // HALO) % 2
    which = lax.shift_right_logical(column, bits)
    entry = column & (slot - 1)
    place = jnp.zeros(shape, F32)
    start = -prior[0]
    for b in range(SALVO_TALLY):
        ramp = jnp.ones(shape, F32)
        if b > 0:
            start = start + sweeps - seams[0, b - 1]
            up = (line - start + 1).astype(F32) / (seams[0, b - 1] + 1).astype(F32)
            ramp = ramp * jnp.clip(up, 0.0, 1.0)
        if b < SALVO_TALLY - 1:
            down = (start + sweeps - line).astype(F32) / (seams[0, b] + 1).astype(F32)
            ramp = ramp * jnp.clip(down, 0.0, 1.0)
        here = (which == part * SALVO_TALLY + b) & (line == start + entry)
        place = jnp.where(here, ramp, place)
    inside = (entry < sweeps) & (line >= 0) & (line < sweep_labels)
    place = jnp.where(inside, place, 0.0).astype(BF16)
    merged = jnp.dot(place, held[...], preferred_element_type=F32)
    out[...] = merged.reshape(out.shape).astype(BF16)


def seam(bursts, weights, drifts, seams, prior, devices):
    sweeps, cells = bursts.shape[3:]
    slot = 16
    while slot < sweeps:
        slot *= 2
    smem = pl.BlockSpec(memory_space=pltpu.SMEM)
    vmem = pl.BlockSpec(memory_space=pltpu.VMEM)
    return pl.pallas_call(
        functools.partial(seam_kernel, sweep_labels=LB * devices),
        out_shape=jax.ShapeDtypeStruct((devices, 2 * HALO, cells), BF16),
        in_specs=[smem, smem, smem, vmem, vmem],
        out_specs=vmem,
        scratch_shapes=[pltpu.VMEM((2 * SALVO_TALLY * slot, cells), BF16)],
    )(drifts, seams, prior, weights, bursts)


def link_kernel(frames, ground, out, wide, table, left, right32, rebuilt):
    dates, _, cells = ground.shape
    windows = frames.shape[0]
    depth = 2 * dates
    span = depth * windows
    chunks = cells // LANES
    rows = ground[...].astype(F32).reshape(dates * 2 * HALO, cells)
    for j in range(chunks):
        wide[j] = rows[:, j * LANES : (j + 1) * LANES]
        for r in range(2 * HALO):
            table[r, j] = wide[j, pl.ds(r, dates, stride=2 * HALO), :]

    def collect(w, carry):
        pixel = frames[pl.ds(w, 1), :]
        low = jnp.broadcast_to(pixel & (LANES - 1), (8, LANES))
        high = jnp.broadcast_to(lax.shift_right_logical(pixel, 7), (8, LANES))
        found = [[jnp.zeros((8, LANES), F32) for _ in range(dates // 8)] for _ in range(2)]
        for t in range(HALO):
            for j in range(chunks):
                here = high == t * chunks + j
                for c in range(2):
                    for g in range(dates // 8):
                        tile = table[c * HALO + t, j, g * 8 : g * 8 + 8, :]
                        taken = jnp.take_along_axis(tile, low, axis=1, mode="promise_in_bounds")
                        found[c][g] = jnp.where(here, taken, found[c][g])
        real = jnp.concatenate(found[0], axis=0)
        imaginary = jnp.concatenate(found[1], axis=0)
        pieces = ((real, 0, 0), (imaginary, 1, 0), (-imaginary, 0, 1), (real, 1, 1))
        for value, c, half in pieces:
            left[w, c * dates : (c + 1) * dates, pl.ds(half * LANES, LANES)] = value.astype(BF16)
            right32[half, pl.ds(c * dates * windows + w, dates, stride=windows), :] = value
        return carry

    lax.fori_loop(0, windows, collect, 0)
    products = lax.dot_general(
        left[...].reshape(span, 2 * LANES),
        jnp.concatenate([right32[0], right32[1]], axis=1).astype(BF16),
        NT,
        preferred_element_type=F32,
    )
    owner = iota((depth, span), 1) & (windows - 1)
    cov = jnp.zeros((depth, span), F32)
    for w in range(windows):
        cov = jnp.where(owner == w, products[w * depth : (w + 1) * depth], cov)
    cov = cov * (1.0 / LOOKS)

    def over_lanes(value):
        total = value[:, :LANES]
        for j in range(1, span // LANES):
            total = total + value[:, j * LANES : (j + 1) * LANES]
        shift = windows
        while shift < LANES:
            total = total + pltpu.roll(total, shift, 1)
            shift *= 2
        return total

    def over_rows(value):
        return jnp.sum(value, axis=0, keepdims=True)

    def spread(value):
        return jnp.concatenate([value] * (span // LANES), axis=1)

    bits = windows.bit_length() - 1
    same = lax.shift_right_logical(iota((depth, span), 1), bits) == iota((depth, span), 0)
    diagonal = jnp.where(same, cov, 0.0)
    by_lane = lax.rsqrt(over_rows(diagonal) + EPSILON)
    by_row = lax.rsqrt(over_lanes(diagonal) + EPSILON)
    gam = (1.0 - SHRINK) * cov * spread(by_row) * by_lane + jnp.where(same, SHRINK, 0.0)

    y = jnp.where(iota((depth, LANES), 0) < dates, 1.0, 0.0)
    scale = jnp.ones((1, LANES), F32)
    for step in range(ITERS // 2):
        line = over_rows(gam * spread(y))
        size = over_lanes(line * line) * (1.0 / dates)
        scale = scale * lax.rsqrt(scale * scale * size + EPSILON)
        y = over_lanes(gam * line)
        size = over_rows(y * y) * (1.0 / dates)
        scale = scale * lax.rsqrt(scale * scale * size + EPSILON)
    linked = (y * scale).astype(BF16).astype(F32)

    factor = 1.0 / math.sqrt(dates)
    for w in range(windows):
        t, at = (w * LOOKS) // cells, (w * LOOKS) % cells
        column = jnp.broadcast_to(linked[:, w : w + 1], (depth, LANES))
        real, imaginary = column[:dates], column[dates:]
        own_real = table[1 + t, at // LANES]
        own_imaginary = table[HALO + 1 + t, at // LANES]
        value_real = over_rows(real * own_real + imaginary * own_imaginary) * factor
        value_imaginary = over_rows(real * own_imaginary - imaginary * own_real) * factor
        value_real = value_real.astype(BF16).astype(F32)
        value_imaginary = value_imaginary.astype(BF16).astype(F32)
        rebuilt[at // LANES, pl.ds(t, dates, stride=2 * LB), :] = (
            value_real * real - value_imaginary * imaginary
        )
        rebuilt[at // LANES, pl.ds(LB + t, dates, stride=2 * LB), :] = (
            value_real * imaginary + value_imaginary * real
        )
    for d in range(dates):
        for j in range(chunks):
            out[d, :, j * LANES : (j + 1) * LANES] = rebuilt[
                j, d * 2 * LB : (d + 1) * 2 * LB, :
            ].astype(BF16)


def link(ground, frames):
    dates, _, cells = ground.shape
    windows = frames.shape[0]
    depth = 2 * dates
    vmem = pl.BlockSpec(memory_space=pltpu.VMEM)
    return pl.pallas_call(
        link_kernel,
        out_shape=jax.ShapeDtypeStruct((dates, 2 * LB, cells), BF16),
        in_specs=[vmem, vmem],
        out_specs=vmem,
        scratch_shapes=[
            pltpu.VMEM((cells // LANES, dates * 2 * HALO, LANES), F32),
            pltpu.VMEM((2 * HALO, cells // LANES, dates, LANES), F32),
            pltpu.VMEM((windows, depth, 2 * LANES), BF16),
            pltpu.VMEM((2, depth * windows, LANES), F32),
            pltpu.VMEM((cells // LANES, dates * 2 * LB, LANES), F32),
        ],
    )(frames, ground)


def coupling_frames(readings, native_picture_elements):
    sample_real = readings[:, 0]
    sample_imaginary = readings[:, 1]

    def pair(left, right):
        return jnp.einsum("dwm,ewm->wde", left, right, preferred_element_type=F32)

    inverse_looks = 1.0 / LOOKS
    covariance_real = (
        pair(sample_real, sample_real) + pair(sample_imaginary, sample_imaginary)
    ) * inverse_looks
    mixed = pair(sample_imaginary, sample_real)
    covariance_imaginary = (mixed - jnp.swapaxes(mixed, 1, 2)) * inverse_looks
    dates = readings.shape[0]
    inverse_root = lax.rsqrt(jnp.diagonal(covariance_real, axis1=1, axis2=2) + EPSILON)
    outer = inverse_root[:, :, None] * inverse_root[:, None, :]
    identity = jnp.eye(dates, dtype=F32)
    coherence_real = (1.0 - SHRINK) * covariance_real * outer + SHRINK * identity
    coherence_imaginary = (1.0 - SHRINK) * covariance_imaginary * outer
    vector_real = jnp.ones(inverse_root.shape, F32)
    vector_imaginary = jnp.zeros(inverse_root.shape, F32)

    def apply_matrix(matrix, vector):
        return jnp.einsum("wde,we->wd", matrix, vector, precision=lax.Precision.HIGHEST)

    for iteration in range(ITERS):
        image_real = apply_matrix(coherence_real, vector_real) - apply_matrix(
            coherence_imaginary, vector_imaginary
        )
        image_imaginary = apply_matrix(coherence_real, vector_imaginary) + apply_matrix(
            coherence_imaginary, vector_real
        )
        power = image_real * image_real + image_imaginary * image_imaginary
        factor = lax.rsqrt(jnp.mean(power, axis=1, keepdims=True) + EPSILON)
        vector_real = image_real * factor
        vector_imaginary = image_imaginary * factor
    coupled_result = jnp.stack([vector_real, vector_imaginary]).astype(BF16)

    def project(history, pixels):
        return jnp.einsum("wd,dwm->wm", history, pixels, preferred_element_type=F32)

    scaling = 1.0 / math.sqrt(dates)
    own_real = native_picture_elements[:, 0]
    own_imaginary = native_picture_elements[:, 1]
    compressed_real = (
        project(coupled_result[0], own_real) + project(coupled_result[1], own_imaginary)
    ) * scaling
    compressed_imaginary = (
        project(coupled_result[0], own_imaginary) - project(coupled_result[1], own_real)
    ) * scaling
    condensed_result = jnp.stack([compressed_real, compressed_imaginary]).astype(BF16)
    return (condensed_result, coupled_result)


def link_plain(ground, frames):
    dates, _, cells = ground.shape
    windows = frames.shape[0]
    extended = ground.reshape(dates, 2, HALO, cells)
    flat = extended.reshape(dates, 2, HALO * cells)
    readings = jnp.take(flat, frames.reshape(-1), axis=2).reshape(dates, 2, windows, LOOKS)
    native = extended[:, :, 1 : LB + 1].reshape(dates, 2, windows, LOOKS)
    condensed_result, coupled_result = coupling_frames(readings, native)
    history_real = coupled_result[0].astype(F32).T[:, :, None]
    history_imaginary = coupled_result[1].astype(F32).T[:, :, None]
    value_real = condensed_result[0].astype(F32)[None]
    value_imaginary = condensed_result[1].astype(F32)[None]
    rebuilt = jnp.stack(
        [
            value_real * history_real - value_imaginary * history_imaginary,
            value_real * history_imaginary + value_imaginary * history_real,
        ],
        axis=1,
    ).astype(BF16)
    return rebuilt.reshape(dates, 2 * LB, cells)


def dft_tables(length, span):
    first, second = np.arange(span)[:, None], np.arange(span)[None, :]
    angle = (first % length) * (second % length) % length * (2.0 * math.pi / length)
    inside = first // length == second // length
    return np.where(inside, np.cos(angle), 0.0), np.where(inside, np.sin(angle), 0.0)


def patch_kernel(range_table, ahead_table, back_table, mine, out, wide):
    blocks, _, cells = mine.shape
    chunks = cells // LANES

    def cut(value, j):
        return value[:, j * LANES : (j + 1) * LANES]

    for b in range(blocks):
        rows = mine[b].astype(F32)
        for j in range(chunks):
            wide[j, b * 2 * LB : (b + 1) * 2 * LB, :] = cut(rows, j)

    def lines_of(c, j):
        pieces = [wide[j, pl.ds(c * LB + t, blocks, stride=2 * LB), :] for t in range(LB)]
        return jnp.concatenate(pieces, axis=0).astype(BF16)

    first = jnp.concatenate(
        [
            jnp.concatenate([lines_of(0, j), lines_of(1, j)], axis=1)
            for j in range(chunks)
        ],
        axis=0,
    )

    def by_chunk(real, imaginary):
        return jnp.concatenate(
            [
                jnp.concatenate([cut(real, j), cut(imaginary, j)], axis=1)
                for j in range(chunks)
            ],
            axis=0,
        )

    def by_line(value, c):
        return jnp.concatenate(
            [cut(value[j * PATCH : (j + 1) * PATCH], c) for j in range(chunks)], axis=1
        )

    table = range_table[...]
    across = jnp.dot(first, table, preferred_element_type=F32).astype(BF16)
    across = jnp.concatenate([by_line(across, 0), by_line(across, 1)], axis=0)
    spectrum = jnp.dot(ahead_table[...], across, preferred_element_type=F32)
    real, imaginary = spectrum[:PATCH], spectrum[PATCH:]
    power = real * real + imaginary * imaginary
    total = jnp.sum(power, axis=0, keepdims=True)
    total = jnp.concatenate([cut(total, j) for j in range(chunks)], axis=0)
    lane = iota(total.shape, 1)
    shift = 1
    while shift < PATCH:
        other = jnp.where(
            (lane & shift) == 0, pltpu.roll(total, LANES - shift, 1), pltpu.roll(total, shift, 1)
        )
        total = total + other
        shift *= 2
    mean = total * (1.0 / (PATCH * PATCH)) + EPSILON
    mean = jnp.concatenate([mean[j : j + 1] for j in range(chunks)], axis=1)
    ramp = jnp.sqrt(jnp.sqrt(power / mean))
    weighted = jnp.concatenate([real * ramp, imaginary * ramp], axis=0).astype(BF16)
    back = jnp.dot(back_table[...], weighted, preferred_element_type=F32).astype(BF16)
    back = by_chunk(back[:PATCH], back[PATCH:])
    final = lax.dot_general(back, table, NT, preferred_element_type=F32)
    final = (final * (1.0 / (PATCH * PATCH))).astype(BF16)
    for c in range(2):
        out[0, c] = by_line(final, c)


def patch_filter(mine, lines):
    cells = mine.shape[2]
    blocks = PATCH // LB
    cosine, sine = dft_tables(PATCH, LANES)
    range_table = np.block([[cosine, -sine], [sine, cosine]])
    cosine, sine = dft_tables(PATCH, PATCH)
    order = np.arange(PATCH).reshape(blocks, LB).T.reshape(-1)
    ahead = np.block([[cosine[:, order], sine[:, order]], [-sine[:, order], cosine[:, order]]])
    back = np.block([[cosine, -sine], [sine, cosine]])
    tables = [jnp.asarray(entry, F32).astype(BF16) for entry in (range_table, ahead, back)]
    return pl.pallas_call(
        patch_kernel,
        grid=(lines // PATCH,),
        out_shape=jax.ShapeDtypeStruct((1, 2, lines, cells), BF16),
        in_specs=[
            pl.BlockSpec((2 * LANES, 2 * LANES), lambda p: (0, 0)),
            pl.BlockSpec((2 * PATCH, 2 * PATCH), lambda p: (0, 0)),
            pl.BlockSpec((2 * PATCH, 2 * PATCH), lambda p: (0, 0)),
            pl.BlockSpec((blocks, 2 * LB, cells), lambda p: (p, 0, 0)),
        ],
        out_specs=pl.BlockSpec((1, 2, PATCH, cells), lambda p: (0, 0, p, 0)),
        scratch_shapes=[pltpu.VMEM((cells // LANES, blocks * 2 * LB, LANES), F32)],
    )(*tables, mine)


def on_device(
    salvo_records, stencil_weights, zone_drifts, seam_sweeps, prior_sweeps, viewing_frames
):
    devices = lax.axis_size("date")
    merged = seam(
        salvo_records, stencil_weights, zone_drifts, seam_sweeps, prior_sweeps, devices
    )
    ground = lax.all_to_all(merged, "date", split_axis=0, concat_axis=0, tiled=True)
    windows = viewing_frames.shape[0]
    fits = devices <= 32 and devices % 16 == 0 and LANES % windows == 0
    rebuilt = (link if fits else link_plain)(ground, viewing_frames)
    mine = lax.all_to_all(rebuilt, "date", split_axis=0, concat_axis=0, tiled=True)
    return patch_filter(mine, LB * devices)


def solution(mesh):
    in_specs = (
        P(("group", "date"), None, None, None, None),
        P(("group", "date"), None, None),
        P(("group", "date"), None),
        P(("group", "date"), None),
        P(("group", "date")),
        P(("group", "date"), None),
    )
    out_specs = P(("group", "date"), None, None, None)
    return jax.shard_map(
        on_device, mesh=mesh, in_specs=in_specs, out_specs=out_specs, check_vma=False
    )
```

time: 116 us -> 44.9 us (0.39)
  other arithmetic: 35.1 us -> 0 us
  blocking collectives: 0 us -> 29.6 us
  matrix products: 22.4 us -> 0 us
  local copies, waits for them, and re-layouts: 19.4 us -> 1.64 us
  starting transfers between devices: 17.4 us -> 0 us
  waiting for transfers between devices: 17 us -> 0 us
  Pallas kernels: 0 us -> 12.6 us
  between operations: 3.85 us -> 0.66 us
    all_to_all x0 -> x2, blocking collectives: none -> 29.6 us  [the longest x1 17.5 us: on_device(): lax.all_to_all(merged, 'date', split_axis=0, concat_axis=0, tiled=True)]
    select_n x4 -> x0, other arithmetic: 27.1 us -> none  [the longest x2 27.1 us: regridding_tableau(): matrix = jnp.where(distance == tap_index, tap_row[tap_index], matrix)]
    dot_general x56 -> x0, matrix products: 22.4 us -> none  [the longest x32 11.8 us: apply_matrix(): jnp.einsum('wde,we->wd', matrix, vector, precision=lax.Precision.HIGHEST)]
    all_to_all x2 -> x0, waiting for transfers between devices: 15.6 us -> none  [the longest x1 7.86 us: on_device(): lax.all_to_all(rebuilt, 'date', split_axis=0, concat_axis=2, tiled=True)[0]]
    all_to_all x2 -> x0, starting transfers between devices: 14.6 us -> none  [the longest x1 7.41 us: on_device(): lax.all_to_all(seamed_picture[None], 'date', split_axis=2, concat_axis=0,...]
    pallas_call x0 -> x3, Pallas kernels: none -> 12.6 us  [the longest x1 6.99 us: link(): pl.pallas_call(link_kernel, out_shape=jax.ShapeDtypeStruct((dates, 2 * LB...]
    gather x3 -> x0, local copies, waits for them, and re-layouts: 8.37 us -> none  [the longest x2 7.75 us: on_device(): jnp.take(flat, viewing_frames.reshape(-1), axis=2)]
    slice x7 -> x0, local copies, waits for them, and re-layouts: 7.17 us -> none  [the longest x2 3.62 us: regridding_tableau(): matrix = jnp.where(distance == tap_index, tap_row[tap_index], matrix)]
  transfers between devices with their start and end apart: 4 -> 0, of which waited for: 3 -> 0; matrix products, arithmetic and copies ran while one was open for 0% -> 0% of each run, Pallas kernels for 0% -> 0%
where the time goes in v1:
time: 44.9 us; the launch traced here: 44.5 us
  blocking collectives  29.6 us (66%)
  Pallas kernels  12.6 us (28%)
  local copies, waits for them, and re-layouts  1.64 us (4%)
  between operations  0.66 us (1%)
    all_to_all x1, blocking collectives, on_device(): lax.all_to_all(merged, 'date', split_axis=0, concat_axis=0, tiled=True)  17.5 us
    all_to_all x1, blocking collectives, on_device(): lax.all_to_all(rebuilt, 'date', split_axis=0, concat_axis=0, tiled=True)  12.1 us
    pallas_call x1, Pallas kernels, link(): pl.pallas_call(link_kernel, out_shape=jax.ShapeDtypeStruct((dates, 2 * LB...  6.99 us
    pallas_call x1, Pallas kernels, seam(): pl.pallas_call(functools.partial(seam_kernel, sweep_labels=LB * devices),...  2.93 us
    pallas_call x1, Pallas kernels, patch_filter(): pl.pallas_call(patch_kernel, grid=(lines // PATCH,), out_shape=jax.ShapeD...  2.73 us
    unnamed x1, local copies, waits for them, and re-layouts  1.64 us

profile of v1, /device:TPU:0, one launch (start us, length us, event | category | flops | bytes accessed | tf_op | source)
XLA Modules:
  0.0 44.5 jit_solution(4208425663769088607)
XLA Ops:
  0.7 1.6 %copy.10.bursts = bf16[1,3,2,13,1024]{4,3,2,1,0:T(8,128)(2,1)} copy(bf16[1,3,2,13,1024]{4,2,3,1,0:T(2,128)(2,1)} %param.9) | data formatting | bytes 319488 | tf_op args[0]
  2.3 2.9 %shard_map.91 = bf16[16,8,1024]{2,1,0:T(8,128)(2,1)} custom-call(s32[1,3]{1,0:T(1,128)} %drifts.1, s32[1,2]{1,0:T(1,128)} %seams.1, s32[1]{0:T(128)S(6)} %copy.11.prior, bf16[1,3,8]{2,1,0:T(4,128)(2,1)} %weights.1, bf16[1,3,2,13,1024]{4,3,2,1,0:T(8,128)(2,1)} %copy.10.bursts), custom_call_target="tpu_custom_call" | custom-call | tf_op jit(solution)/shard_map/pallas_call | solution.py:85
  5.2 17.5 %all_to_all.10.ground = bf16[16,8,1024]{2,1,0:T(8,128)(2,1)} all-to-all(bf16[16,8,1024]{2,1,0:T(8,128)(2,1)} %shard_map.91), channel_id=1, replica_groups=mesh['group'=2,'date'=16] {'date'}, dimensions={0} | all-to-all | bytes 524288 | tf_op jit(solution)/shard_map/all_to_all | solution.py:399
  22.8 7.0 %shard_map.92 = bf16[16,4,1024]{2,1,0:T(4,128)(2,1)} custom-call(s32[16,128]{1,0:T(8,128)} %frames.1, bf16[16,8,1024]{2,1,0:T(8,128)(2,1)} %all_to_all.10.ground), custom_call_target="tpu_custom_call" | custom-call | tf_op jit(solution)/shard_map/pallas_call | solution.py:203
  29.7 12.1 %all_to_all.11.mine = bf16[16,4,1024]{2,1,0:T(4,128)(2,1)} all-to-all(bf16[16,4,1024]{2,1,0:T(4,128)(2,1)} %shard_map.92), channel_id=1, replica_groups=mesh['group'=2,'date'=16] {'date'}, dimensions={0} | all-to-all | bytes 262144 | tf_op jit(solution)/shard_map/all_to_all | solution.py:403
  41.8 2.7 %shard_map.93 = bf16[1,2,32,1024]{3,2,1,0:T(8,128)(2,1)} custom-call(bf16[256,256]{1,0:T(8,128)(2,1)} %constant.15.range_table, bf16[64,64]{1,0:T(8,128)(2,1)} %constant.16.ahead_table, bf16[64,64]{1,0:T(8,128)(2,1)} %constant.17.back_table, bf16[16,4,1024]{2,1,0:T(4,128)(2,1)} %all_to_all.11.mine), custom_call_target="tpu_custom_call" | custom-call | tf_op jit(solution)/shard_map/pallas_call | solution.py:377

commit v2 on v1

--- a/solution.py
+++ b/solution.py
@@ -28,6 +28,10 @@
 
 def iota(shape, axis):
     return lax.broadcasted_iota(jnp.int32, shape, axis)
+
+
+def grant(devices):
+    return pltpu.CompilerParams(vmem_limit_bytes=min(devices, 120) * 2**19)
 
 
 def seam_kernel(drifts, seams, prior, weights, bursts, out, held, *, sweep_labels):
@@ -88,6 +92,7 @@
         in_specs=[smem, smem, smem, vmem, vmem],
         out_specs=vmem,
         scratch_shapes=[pltpu.VMEM((2 * SALVO_TALLY * slot, cells), BF16)],
+        compiler_params=grant(devices),
     )(drifts, seams, prior, weights, bursts)
 
 
@@ -212,6 +217,7 @@
             pltpu.VMEM((2, depth * windows, LANES), F32),
             pltpu.VMEM((cells // LANES, dates * 2 * LB, LANES), F32),
         ],
+        compiler_params=grant(dates),
     )(frames, ground)
 
 
@@ -386,6 +392,7 @@
         ],
         out_specs=pl.BlockSpec((1, 2, PATCH, cells), lambda p: (0, 0, p, 0)),
         scratch_shapes=[pltpu.VMEM((cells // LANES, blocks * 2 * LB, LANES), F32)],
+        compiler_params=grant(lines // LB),
     )(*tables, mine)
 
 

time: 44.9 us -> 38.8 us (0.86)
  Pallas kernels: 12.6 us -> 8.9 us
  blocking collectives: 29.6 us -> 27.9 us
  local copies, waits for them, and re-layouts: 1.64 us -> 1.01 us
    pallas_call x1, Pallas kernels: 6.99 us -> 5.37 us  [link(): pl.pallas_call(link_kernel, out_shape=jax.ShapeDtypeStruct((dates, 2 * LB...]
    all_to_all x1, blocking collectives: 12.1 us -> 10.7 us  [on_device(): lax.all_to_all(rebuilt, 'date', split_axis=0, concat_axis=0, tiled=True)]
    pallas_call x1, Pallas kernels: 2.93 us -> 1.81 us  [seam(): pl.pallas_call(functools.partial(seam_kernel, sweep_labels=LB * devices),...]
    pallas_call x1, Pallas kernels: 2.73 us -> 1.73 us  [patch_filter(): pl.pallas_call(patch_kernel, grid=(lines // PATCH,), out_shape=jax.ShapeD...]
    unnamed x1 -> x15, local copies, waits for them, and re-layouts: 1.64 us -> 1.01 us
where the time goes in v2:
time: 38.8 us; the launch traced here: 38.6 us
  blocking collectives  27.9 us (72%)
  Pallas kernels  8.9 us (23%)
  local copies, waits for them, and re-layouts  1.01 us (3%)
  between operations  0.76 us (2%)
    all_to_all x1, blocking collectives, on_device(): lax.all_to_all(merged, 'date', split_axis=0, concat_axis=0, tiled=True)  17.2 us
    all_to_all x1, blocking collectives, on_device(): lax.all_to_all(rebuilt, 'date', split_axis=0, concat_axis=0, tiled=True)  10.7 us
    pallas_call x1, Pallas kernels, link(): pl.pallas_call(link_kernel, out_shape=jax.ShapeDtypeStruct((dates, 2 * LB...  5.37 us
    pallas_call x1, Pallas kernels, seam(): pl.pallas_call(functools.partial(seam_kernel, sweep_labels=LB * devices),...  1.81 us
    pallas_call x1, Pallas kernels, patch_filter(): pl.pallas_call(patch_kernel, grid=(lines // PATCH,), out_shape=jax.ShapeD...  1.73 us
    unnamed x15, local copies, waits for them, and re-layouts  1.01 us

profile of v2, /device:TPU:0, one launch (start us, length us, event | category | flops | bytes accessed | tf_op | source)
XLA Modules:
  0.0 38.6 jit_solution(15060152073243432083)
XLA Ops:
  0.7 0.0 copy-start.4
  0.7 0.0 copy-start.5
  0.7 0.0 copy-start.6
  0.7 1.0 %copy.10.bursts = bf16[1,3,2,13,1024]{4,3,2,1,0:T(8,128)(2,1)S(1)} copy(bf16[1,3,2,13,1024]{4,2,3,1,0:T(2,128)(2,1)} %param.9) | data formatting | bytes 319488 | tf_op args[0]
  1.7 0.0 copy-done.4
  1.7 0.0 copy-done.5
  1.7 0.0 copy-done.6
  1.7 1.8 %shard_map.91 = bf16[16,8,1024]{2,1,0:T(8,128)(2,1)S(1)} custom-call(s32[1,3]{1,0:T(1,128)S(1)} %copy-done.5, s32[1,2]{1,0:T(1,128)S(1)} %copy-done.6, s32[1]{0:T(128)S(6)} %copy.11.prior, bf16[1,3,8]{2,1,0:T(4,128)(2,1)S(1)} %copy-done.4, bf16[1,3,2,13,1024]{4,3,2,1,0:T(8,128)(2,1)S(1)} %copy.10.bursts), custom_call_target="tpu_custom_call" | custom-call | tf_op jit(solution)/shard_map/pallas_call | solution.py:89
  3.5 0.0 copy-start.3
  3.5 17.2 %all_to_all.10.ground = bf16[16,8,1024]{2,1,0:T(8,128)(2,1)S(1)} all-to-all(bf16[16,8,1024]{2,1,0:T(8,128)(2,1)S(1)} %shard_map.91), channel_id=1, replica_groups=mesh['group'=2,'date'=16] {'date'}, dimensions={0} | all-to-all | bytes 524288 | tf_op jit(solution)/shard_map/all_to_all | solution.py:406
  20.7 0.0 copy-done.3
  20.7 5.4 %shard_map.92 = bf16[16,4,1024]{2,1,0:T(4,128)(2,1)S(1)} custom-call(s32[16,128]{1,0:T(8,128)S(1)} %copy-done.3, bf16[16,8,1024]{2,1,0:T(8,128)(2,1)S(1)} %all_to_all.10.ground), custom_call_target="tpu_custom_call" | custom-call | tf_op jit(solution)/shard_map/pallas_call | solution.py:208
  26.1 0.0 copy-start
  26.1 0.0 copy-start.1
  26.1 0.0 copy-start.2
  26.2 10.7 %all_to_all.11.mine = bf16[16,4,1024]{2,1,0:T(4,128)(2,1)S(1)} all-to-all(bf16[16,4,1024]{2,1,0:T(4,128)(2,1)S(1)} %shard_map.92), channel_id=1, replica_groups=mesh['group'=2,'date'=16] {'date'}, dimensions={0} | all-to-all | bytes 262144 | tf_op jit(solution)/shard_map/all_to_all | solution.py:410
  36.9 0.0 copy-done
  36.9 0.0 copy-done.1
  36.9 0.0 copy-done.2
  36.9 1.7 %shard_map.93 = bf16[1,2,32,1024]{3,2,1,0:T(8,128)(2,1)} custom-call(bf16[256,256]{1,0:T(8,128)(2,1)S(1)} %copy-done, bf16[64,64]{1,0:T(8,128)(2,1)S(1)} %copy-done.2, bf16[64,64]{1,0:T(8,128)(2,1)S(1)} %copy-done.1, bf16[16,4,1024]{2,1,0:T(4,128)(2,1)S(1)} %all_to_all.11.mine), custom_call_target="tpu_custom_call" | custom-call | tf_op jit(solution)/shard_map/pallas_call | solution.py:383
Async XLA Ops:
  0.7 1.0 %copy-start.4 = (bf16[1,3,8]{2,1,0:T(4,128)(2,1)S(1)}, bf16[1,3,8]{2,1,0:T(4,128)(2,1)}, u32[]{:S(2)}) copy-start(bf16[1,3,8]{2,1,0:T(4,128)(2,1)} %weights.1) | copy-start | bytes 148
  0.7 1.0 %copy-start.5 = (s32[1,3]{1,0:T(1,128)S(1)}, s32[1,3]{1,0:T(1,128)}, u32[]{:S(2)}) copy-start(s32[1,3]{1,0:T(1,128)} %drifts.1) | copy-start | bytes 40
  0.7 1.0 %copy-start.6 = (s32[1,2]{1,0:T(1,128)S(1)}, s32[1,2]{1,0:T(1,128)}, u32[]{:S(2)}) copy-start(s32[1,2]{1,0:T(1,128)} %seams.1) | copy-start | bytes 28
  3.5 17.2 %copy-start.3 = (s32[16,128]{1,0:T(8,128)S(1)}, s32[16,128]{1,0:T(8,128)}, u32[]{:S(2)}) copy-start(s32[16,128]{1,0:T(8,128)} %frames.1) | copy-start | bytes 24580
  26.1 10.7 %copy-start = (bf16[256,256]{1,0:T(8,128)(2,1)S(1)}, bf16[256,256]{1,0:T(8,128)(2,1)}, u32[]{:S(2)}) copy-start(bf16[256,256]{1,0:T(8,128)(2,1)} %constant.15.range_table) | copy-start | bytes 393220
  26.1 10.7 %copy-start.1 = (bf16[64,64]{1,0:T(8,128)(2,1)S(1)}, bf16[64,64]{1,0:T(8,128)(2,1)}, u32[]{:S(2)}) copy-start(bf16[64,64]{1,0:T(8,128)(2,1)} %constant.17.back_table) | copy-start | bytes 24580
  26.1 10.7 %copy-start.2 = (bf16[64,64]{1,0:T(8,128)(2,1)S(1)}, bf16[64,64]{1,0:T(8,128)(2,1)}, u32[]{:S(2)}) copy-start(bf16[64,64]{1,0:T(8,128)(2,1)} %constant.16.ahead_table) | copy-start | bytes 24580

commit v3 on v2

--- a/solution.py
+++ b/solution.py
@@ -34,32 +34,59 @@
     return pltpu.CompilerParams(vmem_limit_bytes=min(devices, 120) * 2**19)
 
 
-def seam_kernel(drifts, seams, prior, weights, bursts, out, held, *, sweep_labels):
-    sweeps, cells = bursts.shape[3:]
-    slot = held.shape[0] // (2 * SALVO_TALLY)
+def seam_kernel(*refs, sweep_labels):
+    prior, sources, out = refs[0], refs[1:5], refs[5]
+    (drifts, seams, weights, bursts), (wide, done) = refs[6:10], refs[10:]
+    copies = [
+        pltpu.make_async_copy(source, target, done.at[n])
+        for n, (source, target) in enumerate(zip(sources, refs[6:10]))
+    ]
+    for copy in copies:
+        copy.start()
+    for copy in copies:
+        copy.wait()
+    sweeps, _, cells = bursts.shape[2:]
+    slot = wide.shape[0] // SALVO_TALLY
     span = cells + LANES
-    held[...] = jnp.zeros(held.shape, held.dtype)
+    chunks = cells // LANES
+    for b in range(SALVO_TALLY):
+        for i in range(sweeps):
+            wide[b * slot + 2 * i : b * slot + 2 * i + 2, :] = bursts[0, b, i].astype(F32)
+        if 2 * sweeps < slot:
+            wide[b * slot + 2 * sweeps : (b + 1) * slot, :] = jnp.zeros(
+                (slot - 2 * sweeps, cells), F32
+            )
     taps = weights[0].astype(F32)
+    row, column = iota((LANES, LANES), 0), iota((LANES, LANES), 1)
+    resampled = []
     for b in range(SALVO_TALLY):
         first = span + (STENCIL_WEIGHTS // 2 - 1) - drifts[0, b]
         first = jnp.where(first >= span, first - span, first)
-        for c in range(2):
-            row = jnp.concatenate(
-                [bursts[0, b, c].astype(F32), jnp.zeros((sweeps, LANES), F32)], axis=1
-            )
-            row = pltpu.roll(row, first, 1)
-            total = row * taps[b : b + 1, 0:1]
-            for k in range(1, STENCIL_WEIGHTS):
-                total = total + pltpu.roll(row, span - k, 1) * taps[b : b + 1, k : k + 1]
-            base = (c * SALVO_TALLY + b) * slot
-            held[base : base + sweeps, :] = total[:, :cells].astype(BF16)
-    shape = (out.shape[0] * 2 * HALO, held.shape[0])
+        rotated = jnp.concatenate(
+            [wide[b * slot : (b + 1) * slot, :], jnp.zeros((slot, LANES), F32)], axis=1
+        )
+        rotated = pltpu.roll(rotated, first, 1).astype(BF16)
+        rotated = jnp.concatenate(
+            [rotated[:, j * LANES : (j + 2) * LANES] for j in range(chunks)], axis=0
+        )
+        band = jnp.zeros((LANES, LANES), F32)
+        for k in range(STENCIL_WEIGHTS):
+            band = jnp.where(column == (LANES - k) % LANES, taps[b : b + 1, k : k + 1], band)
+        band = pltpu.roll(band, 0, 1, stride=1, stride_axis=0)
+        band = jnp.concatenate(
+            [jnp.where(column <= row, band, 0.0), jnp.where(column > row, band, 0.0)], axis=0
+        )
+        total = jnp.dot(rotated, band.astype(BF16), preferred_element_type=F32).astype(BF16)
+        resampled.append(
+            jnp.concatenate([total[j * slot : (j + 1) * slot] for j in range(chunks)], axis=1)
+        )
+    shape = (out.shape[0] * 2 * HALO, SALVO_TALLY * slot)
     bits = slot.bit_length() - 1
     row, column = iota(shape, 0), iota(shape, 1)
     line = (row // (2 * HALO)) * LB - 1 + row % HALO
     part = (row // HALO) % 2
     which = lax.shift_right_logical(column, bits)
-    entry = column & (slot - 1)
+    entry = lax.shift_right_logical(column & (slot - 1), 1)
     place = jnp.zeros(shape, F32)
     start = -prior[0]
     for b in range(SALVO_TALLY):
@@ -71,29 +98,38 @@
         if b < SALVO_TALLY - 1:
             down = (start + sweeps - line).astype(F32) / (seams[0, b] + 1).astype(F32)
             ramp = ramp * jnp.clip(down, 0.0, 1.0)
-        here = (which == part * SALVO_TALLY + b) & (line == start + entry)
-        place = jnp.where(here, ramp, place)
-    inside = (entry < sweeps) & (line >= 0) & (line < sweep_labels)
+        place = jnp.where((which == b) & (line == start + entry), ramp, place)
+    inside = (entry < sweeps) & (column & 1 == part) & (line >= 0) & (line < sweep_labels)
     place = jnp.where(inside, place, 0.0).astype(BF16)
-    merged = jnp.dot(place, held[...], preferred_element_type=F32)
+    merged = jnp.dot(place, jnp.concatenate(resampled, axis=0), preferred_element_type=F32)
     out[...] = merged.reshape(out.shape).astype(BF16)
 
 
 def seam(bursts, weights, drifts, seams, prior, devices):
     sweeps, cells = bursts.shape[3:]
     slot = 16
-    while slot < sweeps:
+    while slot < 2 * sweeps:
         slot *= 2
-    smem = pl.BlockSpec(memory_space=pltpu.SMEM)
-    vmem = pl.BlockSpec(memory_space=pltpu.VMEM)
+    bursts = bursts.transpose(0, 1, 3, 2, 4)
+    arrays = (drifts, seams, weights, bursts)
     return pl.pallas_call(
         functools.partial(seam_kernel, sweep_labels=LB * devices),
         out_shape=jax.ShapeDtypeStruct((devices, 2 * HALO, cells), BF16),
-        in_specs=[smem, smem, smem, vmem, vmem],
-        out_specs=vmem,
-        scratch_shapes=[pltpu.VMEM((2 * SALVO_TALLY * slot, cells), BF16)],
+        in_specs=[
+            pl.BlockSpec(memory_space=pltpu.SMEM),
+            *[pl.BlockSpec(memory_space=pltpu.HBM)] * len(arrays),
+        ],
+        out_specs=pl.BlockSpec(memory_space=pltpu.VMEM),
+        scratch_shapes=[
+            pltpu.SMEM(drifts.shape, jnp.int32),
+            pltpu.SMEM(seams.shape, jnp.int32),
+            pltpu.VMEM(weights.shape, BF16),
+            pltpu.VMEM(bursts.shape, BF16),
+            pltpu.VMEM((SALVO_TALLY * slot, cells), F32),
+            pltpu.SemaphoreType.DMA((len(arrays),)),
+        ],
         compiler_params=grant(devices),
-    )(drifts, seams, prior, weights, bursts)
+    )(prior, *[pltpu.with_memory_space_constraint(x, pltpu.HBM) for x in arrays])
 
 
 def link_kernel(frames, ground, out, wide, table, left, right32, rebuilt):
@@ -105,31 +141,44 @@
     rows = ground[...].astype(F32).reshape(dates * 2 * HALO, cells)
     for j in range(chunks):
         wide[j] = rows[:, j * LANES : (j + 1) * LANES]
-        for r in range(2 * HALO):
-            table[r, j] = wide[j, pl.ds(r, dates, stride=2 * HALO), :]
-
-    def collect(w, carry):
-        pixel = frames[pl.ds(w, 1), :]
-        low = jnp.broadcast_to(pixel & (LANES - 1), (8, LANES))
-        high = jnp.broadcast_to(lax.shift_right_logical(pixel, 7), (8, LANES))
-        found = [[jnp.zeros((8, LANES), F32) for _ in range(dates // 8)] for _ in range(2)]
-        for t in range(HALO):
-            for j in range(chunks):
-                here = high == t * chunks + j
-                for c in range(2):
-                    for g in range(dates // 8):
-                        tile = table[c * HALO + t, j, g * 8 : g * 8 + 8, :]
-                        taken = jnp.take_along_axis(tile, low, axis=1, mode="promise_in_bounds")
-                        found[c][g] = jnp.where(here, taken, found[c][g])
-        real = jnp.concatenate(found[0], axis=0)
-        imaginary = jnp.concatenate(found[1], axis=0)
-        pieces = ((real, 0, 0), (imaginary, 1, 0), (-imaginary, 0, 1), (real, 1, 1))
-        for value, c, half in pieces:
-            left[w, c * dates : (c + 1) * dates, pl.ds(half * LANES, LANES)] = value.astype(BF16)
-            right32[half, pl.ds(c * dates * windows + w, dates, stride=windows), :] = value
-        return carry
-
-    lax.fori_loop(0, windows, collect, 0)
+
+    def pixels(c, t, j):
+        return wide[j, pl.ds(c * HALO + t, dates, stride=2 * HALO), :]
+
+    segments = HALO * chunks // 2
+    for t in range(HALO):
+        for j in range(chunks):
+            at = (t * (chunks // 2) + j // 2) * depth
+            lanes = pl.ds((j % 2) * LANES, LANES)
+            for c in range(2):
+                table[at + c * dates : at + (c + 1) * dates, lanes] = pixels(c, t, j).astype(BF16)
+
+    places = [
+        (iota((16, LANES), 0) + 16 * n).astype(F32).astype(BF16) for n in range(2 * LANES // 16)
+    ]
+    one, zero = jnp.ones((16, LANES), BF16), jnp.zeros((16, LANES), BF16)
+    for first in range(0, windows, 2):
+        marks, highs = [], []
+        for w in range(first, first + 2):
+            pixel = frames[w : w + 1, :]
+            low = jnp.broadcast_to(pixel & (2 * LANES - 1), (16, LANES)).astype(F32).astype(BF16)
+            marks.append(
+                jnp.concatenate([jnp.where(low == place, one, zero) for place in places], axis=0)
+            )
+            highs.append(lax.shift_right_logical(pixel, 8))
+        high = jnp.broadcast_to(jnp.concatenate(highs, axis=1), (depth, 2 * LANES))
+        taken = jnp.dot(
+            table[...], jnp.concatenate(marks, axis=1), preferred_element_type=F32
+        )
+        found = taken[:depth]
+        for s in range(1, segments):
+            found = jnp.where(high == s, taken[s * depth : (s + 1) * depth], found)
+        for w in range(first, first + 2):
+            value = found[:, (w - first) * LANES : (w - first + 1) * LANES]
+            turned = jnp.concatenate([-value[dates:], value[:dates]], axis=0)
+            for half, piece in enumerate((value, turned)):
+                left[w, :, half * LANES : (half + 1) * LANES] = piece.astype(BF16)
+                right32[half, pl.ds(w, depth, stride=windows), :] = piece
     products = lax.dot_general(
         left[...].reshape(span, 2 * LANES),
         jnp.concatenate([right32[0], right32[1]], axis=1).astype(BF16),
@@ -181,8 +230,8 @@
         t, at = (w * LOOKS) // cells, (w * LOOKS) % cells
         column = jnp.broadcast_to(linked[:, w : w + 1], (depth, LANES))
         real, imaginary = column[:dates], column[dates:]
-        own_real = table[1 + t, at // LANES]
-        own_imaginary = table[HALO + 1 + t, at // LANES]
+        own_real = pixels(0, 1 + t, at // LANES)
+        own_imaginary = pixels(1, 1 + t, at // LANES)
         value_real = over_rows(real * own_real + imaginary * own_imaginary) * factor
         value_imaginary = over_rows(real * own_imaginary - imaginary * own_real) * factor
         value_real = value_real.astype(BF16).astype(F32)
@@ -212,7 +261,7 @@
         out_specs=vmem,
         scratch_shapes=[
             pltpu.VMEM((cells // LANES, dates * 2 * HALO, LANES), F32),
-            pltpu.VMEM((2 * HALO, cells // LANES, dates, LANES), F32),
+            pltpu.VMEM((HALO * cells // (2 * LANES) * depth, 2 * LANES), BF16),
             pltpu.VMEM((windows, depth, 2 * LANES), BF16),
             pltpu.VMEM((2, depth * windows, LANES), F32),
             pltpu.VMEM((cells // LANES, dates * 2 * LB, LANES), F32),
@@ -405,7 +454,8 @@
     )
     ground = lax.all_to_all(merged, "date", split_axis=0, concat_axis=0, tiled=True)
     windows = viewing_frames.shape[0]
-    fits = devices <= 32 and devices % 16 == 0 and LANES % windows == 0
+    fits = devices <= 32 and devices % 16 == 0 and windows % 2 == 0 and LANES % windows == 0
+    fits = fits and salvo_records.shape[4] % (2 * LANES) == 0
     rebuilt = (link if fits else link_plain)(ground, viewing_frames)
     mine = lax.all_to_all(rebuilt, "date", split_axis=0, concat_axis=0, tiled=True)
     return patch_filter(mine, LB * devices)

time: 38.8 us -> 34.9 us (0.90)
  Pallas kernels: 8.9 us -> 6.01 us
  local copies, waits for them, and re-layouts: 1.01 us -> 0.03 us
    pallas_call x1, Pallas kernels: 5.37 us -> 2.63 us  [link(): pl.pallas_call(link_kernel, out_shape=jax.ShapeDtypeStruct((dates, 2 * LB...]
    unnamed x15 -> x8, local copies, waits for them, and re-layouts: 1.01 us -> 0.03 us
where the time goes in v3:
time: 34.9 us; the launch traced here: 34.7 us
  blocking collectives  27.9 us (80%)
  Pallas kernels  6.01 us (17%)
  between operations  0.71 us (2%)
    all_to_all x1, blocking collectives, on_device(): lax.all_to_all(merged, 'date', split_axis=0, concat_axis=0, tiled=True)  17.2 us
    all_to_all x1, blocking collectives, on_device(): lax.all_to_all(rebuilt, 'date', split_axis=0, concat_axis=0, tiled=True)  10.7 us
    pallas_call x1, Pallas kernels, link(): pl.pallas_call(link_kernel, out_shape=jax.ShapeDtypeStruct((dates, 2 * LB...  2.63 us
    pallas_call x1, Pallas kernels, patch_filter(): pl.pallas_call(patch_kernel, grid=(lines // PATCH,), out_shape=jax.ShapeD...  1.73 us
    pallas_call x1, Pallas kernels, seam(): pl.pallas_call(functools.partial(seam_kernel, sweep_labels=LB * devices),...  1.66 us

profile of v3, /device:TPU:0, one launch (start us, length us, event | category | flops | bytes accessed | tf_op | source)
XLA Modules:
  0.0 34.7 jit_solution(2732184792189929165)
XLA Ops:
  0.7 1.7 %shard_map.91 = bf16[16,8,1024]{2,1,0:T(8,128)(2,1)S(1)} custom-call(s32[1]{0:T(128)S(6)} %copy.10.refs_0_, s32[1,3]{1,0:T(1,128)} %refs_1_.1, s32[1,2]{1,0:T(1,128)} %refs_2_.1, bf16[1,3,8]{2,1,0:T(4,128)(2,1)} %refs_3_.1, bf16[1,3,13,2,1024]{4,3,2,1,0:T(2,128)(2,1)} %bitcast.1), custom_call_target="tpu_custom_call" | custom-call | tf_op jit(solution)/shard_map/pallas_call | solution.py:115
  2.3 0.0 copy-start.3
  2.3 17.2 %all_to_all.10.ground = bf16[16,8,1024]{2,1,0:T(8,128)(2,1)S(1)} all-to-all(bf16[16,8,1024]{2,1,0:T(8,128)(2,1)S(1)} %shard_map.91), channel_id=1, replica_groups=mesh['group'=2,'date'=16] {'date'}, dimensions={0} | all-to-all | bytes 524288 | tf_op jit(solution)/shard_map/all_to_all | solution.py:455
  19.6 0.0 copy-done.3
  19.6 2.6 %shard_map.92 = bf16[16,4,1024]{2,1,0:T(4,128)(2,1)S(1)} custom-call(s32[16,128]{1,0:T(8,128)S(1)} %copy-done.3, bf16[16,8,1024]{2,1,0:T(8,128)(2,1)S(1)} %all_to_all.10.ground), custom_call_target="tpu_custom_call" | custom-call | tf_op jit(solution)/shard_map/pallas_call | solution.py:257
  22.2 0.0 copy-start
  22.2 0.0 copy-start.1
  22.2 0.0 copy-start.2
  22.2 10.7 %all_to_all.11.mine = bf16[16,4,1024]{2,1,0:T(4,128)(2,1)S(1)} all-to-all(bf16[16,4,1024]{2,1,0:T(4,128)(2,1)S(1)} %shard_map.92), channel_id=1, replica_groups=mesh['group'=2,'date'=16] {'date'}, dimensions={0} | all-to-all | bytes 262144 | tf_op jit(solution)/shard_map/all_to_all | solution.py:460
  32.9 0.0 copy-done
  32.9 0.0 copy-done.1
  32.9 0.0 copy-done.2
  33.0 1.7 %shard_map.93 = bf16[1,2,32,1024]{3,2,1,0:T(8,128)(2,1)} custom-call(bf16[256,256]{1,0:T(8,128)(2,1)S(1)} %copy-done, bf16[64,64]{1,0:T(8,128)(2,1)S(1)} %copy-done.2, bf16[64,64]{1,0:T(8,128)(2,1)S(1)} %copy-done.1, bf16[16,4,1024]{2,1,0:T(4,128)(2,1)S(1)} %all_to_all.11.mine), custom_call_target="tpu_custom_call" | custom-call | tf_op jit(solution)/shard_map/pallas_call | solution.py:432
Async XLA Ops:
  2.3 17.2 %copy-start.3 = (s32[16,128]{1,0:T(8,128)S(1)}, s32[16,128]{1,0:T(8,128)}, u32[]{:S(2)}) copy-start(s32[16,128]{1,0:T(8,128)} %frames.1) | copy-start | bytes 24580
  22.2 10.8 %copy-start = (bf16[256,256]{1,0:T(8,128)(2,1)S(1)}, bf16[256,256]{1,0:T(8,128)(2,1)}, u32[]{:S(2)}) copy-start(bf16[256,256]{1,0:T(8,128)(2,1)} %constant.15.range_table) | copy-start | bytes 393220
  22.2 10.7 %copy-start.1 = (bf16[64,64]{1,0:T(8,128)(2,1)S(1)}, bf16[64,64]{1,0:T(8,128)(2,1)}, u32[]{:S(2)}) copy-start(bf16[64,64]{1,0:T(8,128)(2,1)} %constant.17.back_table) | copy-start | bytes 24580
  22.2 10.7 %copy-start.2 = (bf16[64,64]{1,0:T(8,128)(2,1)S(1)}, bf16[64,64]{1,0:T(8,128)(2,1)}, u32[]{:S(2)}) copy-start(bf16[64,64]{1,0:T(8,128)(2,1)} %constant.16.ahead_table) | copy-start | bytes 24580

commit v4 on v3

--- a/solution.py
+++ b/solution.py
@@ -16,9 +16,12 @@
 ITERS = 8
 PATCH = 32
 LANES = 128
+SEGMENT = 512
+BATCH = 8
 
 EPSILON = 1e-06
 SHRINK = 0.05
+SMALLEST = float(np.finfo(np.float32).tiny)
 
 HALO = LB + 2
 F32 = jnp.float32
@@ -132,121 +135,159 @@
     )(prior, *[pltpu.with_memory_space_constraint(x, pltpu.HBM) for x in arrays])
 
 
-def link_kernel(frames, ground, out, wide, table, left, right32, rebuilt):
+def link_kernel(frames, ground, out, wide, right32, gam, rebuilt):
     dates, _, cells = ground.shape
     windows = frames.shape[0]
     depth = 2 * dates
     span = depth * windows
     chunks = cells // LANES
-    rows = ground[...].astype(F32).reshape(dates * 2 * HALO, cells)
-    for j in range(chunks):
-        wide[j] = rows[:, j * LANES : (j + 1) * LANES]
+    pitch = 2 * HALO + 1
+    for d in range(dates):
+        rows = ground[d].astype(F32)
+        for j in range(chunks):
+            wide[j, d * pitch : d * pitch + 2 * HALO, :] = rows[:, j * LANES : (j + 1) * LANES]
 
     def pixels(c, t, j):
-        return wide[j, pl.ds(c * HALO + t, dates, stride=2 * HALO), :]
-
-    segments = HALO * chunks // 2
-    for t in range(HALO):
-        for j in range(chunks):
-            at = (t * (chunks // 2) + j // 2) * depth
-            lanes = pl.ds((j % 2) * LANES, LANES)
-            for c in range(2):
-                table[at + c * dates : at + (c + 1) * dates, lanes] = pixels(c, t, j).astype(BF16)
-
-    places = [
-        (iota((16, LANES), 0) + 16 * n).astype(F32).astype(BF16) for n in range(2 * LANES // 16)
-    ]
+        return wide[j, pl.ds(c * HALO + t, dates, stride=pitch), :]
+
+    per = SEGMENT // LANES
+    segments = HALO * chunks // per
+    table = jnp.concatenate(
+        [
+            jnp.concatenate(
+                [
+                    jnp.concatenate(
+                        [pixels(c, *divmod(s * per + n, chunks)) for n in range(per)], axis=1
+                    )
+                    for c in range(2)
+                ],
+                axis=0,
+            ).astype(BF16)
+            for s in range(segments)
+        ],
+        axis=0,
+    )
+
+    half = SEGMENT // 2
+    places = [(iota((16, LANES), 0) + 16 * n).astype(F32).astype(BF16) for n in range(half // 16)]
     one, zero = jnp.ones((16, LANES), BF16), jnp.zeros((16, LANES), BF16)
-    for first in range(0, windows, 2):
+
+    values = []
+    batch = min(BATCH, windows)
+    for first in range(0, windows, batch):
         marks, highs = [], []
-        for w in range(first, first + 2):
+        for w in range(first, first + batch):
             pixel = frames[w : w + 1, :]
-            low = jnp.broadcast_to(pixel & (2 * LANES - 1), (16, LANES)).astype(F32).astype(BF16)
+            low = pixel & (half - 1)
+            upper = (pixel & half) == half
+            keys = [jnp.where(upper, -1, low), jnp.where(upper, low, -1)]
+            keys = [jnp.broadcast_to(key, (16, LANES)).astype(F32).astype(BF16) for key in keys]
             marks.append(
-                jnp.concatenate([jnp.where(low == place, one, zero) for place in places], axis=0)
+                jnp.concatenate(
+                    [jnp.where(key == place, one, zero) for key in keys for place in places],
+                    axis=0,
+                )
             )
-            highs.append(lax.shift_right_logical(pixel, 8))
-        high = jnp.broadcast_to(jnp.concatenate(highs, axis=1), (depth, 2 * LANES))
-        taken = jnp.dot(
-            table[...], jnp.concatenate(marks, axis=1), preferred_element_type=F32
-        )
+            highs.append(lax.shift_right_logical(pixel, SEGMENT.bit_length() - 1))
+        high = jnp.broadcast_to(jnp.concatenate(highs, axis=1), (depth, batch * LANES))
+        taken = jnp.dot(table, jnp.concatenate(marks, axis=1), preferred_element_type=F32)
         found = taken[:depth]
         for s in range(1, segments):
             found = jnp.where(high == s, taken[s * depth : (s + 1) * depth], found)
-        for w in range(first, first + 2):
-            value = found[:, (w - first) * LANES : (w - first + 1) * LANES]
-            turned = jnp.concatenate([-value[dates:], value[:dates]], axis=0)
-            for half, piece in enumerate((value, turned)):
-                left[w, :, half * LANES : (half + 1) * LANES] = piece.astype(BF16)
-                right32[half, pl.ds(w, depth, stride=windows), :] = piece
+        values.extend(found[:, n * LANES : (n + 1) * LANES] for n in range(batch))
+    left = []
+    for w, value in enumerate(values):
+        turned = jnp.concatenate([-value[dates:], value[:dates]], axis=0)
+        left.append(jnp.concatenate([value[:dates], turned[:dates]], axis=1).astype(BF16))
+        for n, piece in enumerate((value, turned)):
+            right32[n, pl.ds(w, depth, stride=windows + 1), :] = piece
     products = lax.dot_general(
-        left[...].reshape(span, 2 * LANES),
-        jnp.concatenate([right32[0], right32[1]], axis=1).astype(BF16),
+        jnp.concatenate(left, axis=0),
+        jnp.concatenate(
+            [
+                jnp.concatenate(
+                    [right32[n, at : at + windows].astype(BF16) for n in range(2)], axis=1
+                )
+                for at in range(0, depth * (windows + 1), windows + 1)
+            ],
+            axis=0,
+        ),
         NT,
         preferred_element_type=F32,
     )
-    owner = iota((depth, span), 1) & (windows - 1)
-    cov = jnp.zeros((depth, span), F32)
-    for w in range(windows):
-        cov = jnp.where(owner == w, products[w * depth : (w + 1) * depth], cov)
+    owner = iota((dates, span), 1) & (windows - 1)
+    cov = products[:dates]
+    for w in range(1, windows):
+        cov = jnp.where(owner == w, products[w * dates : (w + 1) * dates], cov)
     cov = cov * (1.0 / LOOKS)
 
-    def over_lanes(value):
-        total = value[:, :LANES]
-        for j in range(1, span // LANES):
-            total = total + value[:, j * LANES : (j + 1) * LANES]
-        shift = windows
-        while shift < LANES:
-            total = total + pltpu.roll(total, shift, 1)
-            shift *= 2
-        return total
+    column = []
+    for k in range(depth):
+        tile, at = divmod(k * windows, LANES)
+        entry = cov[:, tile * LANES : (tile + 1) * LANES]
+        column.append(pltpu.roll(entry, LANES - at, 1) if at else entry)
+    row = iota((dates, LANES), 0)
+    power = column[0]
+    for d in range(1, dates):
+        power = jnp.where(row == d, column[d], power)
+    inverse = lax.rsqrt(power + EPSILON)
+    for k in range(depth):
+        e = k % dates
+        entry = (1.0 - SHRINK) * column[k] * inverse * inverse[e : e + 1]
+        if k < dates:
+            entry = entry + jnp.where(row == e, SHRINK, 0.0)
+        gam[k] = entry
+
+    def tree(terms):
+        while len(terms) > 1:
+            terms = [terms[n] + terms[n + 1] for n in range(0, len(terms), 2)]
+        return terms[0]
+
+    scale = jnp.ones((1, LANES), F32)
+    real = tree([gam[e] for e in range(dates)])
+    imaginary = -tree([gam[dates + e] for e in range(dates)])
+    for step in range(ITERS):
+        if step:
+            reals = [real[e : e + 1] for e in range(dates)]
+            imaginaries = [imaginary[e : e + 1] for e in range(dates)]
+            real = tree(
+                [gam[e] * reals[e] + gam[dates + e] * imaginaries[e] for e in range(dates)]
+            )
+            imaginary = tree(
+                [gam[e] * imaginaries[e] - gam[dates + e] * reals[e] for e in range(dates)]
+            )
+        size = jnp.sum(real * real + imaginary * imaginary, axis=0, keepdims=True)
+        scale = scale * lax.rsqrt(scale * scale * (size * (1.0 / dates)) + EPSILON)
+    linked_real = (real * scale).astype(BF16).astype(F32)
+    linked_imaginary = (imaginary * scale).astype(BF16).astype(F32)
 
     def over_rows(value):
         return jnp.sum(value, axis=0, keepdims=True)
-
-    def spread(value):
-        return jnp.concatenate([value] * (span // LANES), axis=1)
-
-    bits = windows.bit_length() - 1
-    same = lax.shift_right_logical(iota((depth, span), 1), bits) == iota((depth, span), 0)
-    diagonal = jnp.where(same, cov, 0.0)
-    by_lane = lax.rsqrt(over_rows(diagonal) + EPSILON)
-    by_row = lax.rsqrt(over_lanes(diagonal) + EPSILON)
-    gam = (1.0 - SHRINK) * cov * spread(by_row) * by_lane + jnp.where(same, SHRINK, 0.0)
-
-    y = jnp.where(iota((depth, LANES), 0) < dates, 1.0, 0.0)
-    scale = jnp.ones((1, LANES), F32)
-    for step in range(ITERS // 2):
-        line = over_rows(gam * spread(y))
-        size = over_lanes(line * line) * (1.0 / dates)
-        scale = scale * lax.rsqrt(scale * scale * size + EPSILON)
-        y = over_lanes(gam * line)
-        size = over_rows(y * y) * (1.0 / dates)
-        scale = scale * lax.rsqrt(scale * scale * size + EPSILON)
-    linked = (y * scale).astype(BF16).astype(F32)
 
     factor = 1.0 / math.sqrt(dates)
     for w in range(windows):
         t, at = (w * LOOKS) // cells, (w * LOOKS) % cells
-        column = jnp.broadcast_to(linked[:, w : w + 1], (depth, LANES))
-        real, imaginary = column[:dates], column[dates:]
+        real = jnp.broadcast_to(linked_real[:, w : w + 1], (dates, LANES))
+        imaginary = jnp.broadcast_to(linked_imaginary[:, w : w + 1], (dates, LANES))
         own_real = pixels(0, 1 + t, at // LANES)
         own_imaginary = pixels(1, 1 + t, at // LANES)
         value_real = over_rows(real * own_real + imaginary * own_imaginary) * factor
         value_imaginary = over_rows(real * own_imaginary - imaginary * own_real) * factor
         value_real = value_real.astype(BF16).astype(F32)
         value_imaginary = value_imaginary.astype(BF16).astype(F32)
-        rebuilt[at // LANES, pl.ds(t, dates, stride=2 * LB), :] = (
-            value_real * real - value_imaginary * imaginary
-        )
-        rebuilt[at // LANES, pl.ds(LB + t, dates, stride=2 * LB), :] = (
-            value_real * imaginary + value_imaginary * real
-        )
+        side, tile = divmod(at // LANES, chunks // 2)
+        for c, value in enumerate(
+            (
+                value_real * real - value_imaginary * imaginary,
+                value_real * imaginary + value_imaginary * real,
+            )
+        ):
+            r = (c * LB + t) * 2 + side
+            rebuilt[tile, pl.ds(r, dates, stride=4 * LB + 1), :] = value
     for d in range(dates):
-        for j in range(chunks):
-            out[d, :, j * LANES : (j + 1) * LANES] = rebuilt[
-                j, d * 2 * LB : (d + 1) * 2 * LB, :
-            ].astype(BF16)
+        for j in range(chunks // 2):
+            at = d * (4 * LB + 1)
+            out[d, :, j * LANES : (j + 1) * LANES] = rebuilt[j, at : at + 4 * LB].astype(BF16)
 
 
 def link(ground, frames):
@@ -256,15 +297,14 @@
     vmem = pl.BlockSpec(memory_space=pltpu.VMEM)
     return pl.pallas_call(
         link_kernel,
-        out_shape=jax.ShapeDtypeStruct((dates, 2 * LB, cells), BF16),
+        out_shape=jax.ShapeDtypeStruct((dates, 4 * LB, cells // 2), BF16),
         in_specs=[vmem, vmem],
         out_specs=vmem,
         scratch_shapes=[
-            pltpu.VMEM((cells // LANES, dates * 2 * HALO, LANES), F32),
-            pltpu.VMEM((HALO * cells // (2 * LANES) * depth, 2 * LANES), BF16),
-            pltpu.VMEM((windows, depth, 2 * LANES), BF16),
-            pltpu.VMEM((2, depth * windows, LANES), F32),
-            pltpu.VMEM((cells // LANES, dates * 2 * LB, LANES), F32),
+            pltpu.VMEM((cells // LANES, dates * (2 * HALO + 1), LANES), F32),
+            pltpu.VMEM((2, depth * (windows + 1), LANES), F32),
+            pltpu.VMEM((depth, dates, LANES), F32),
+            pltpu.VMEM((cells // (2 * LANES), dates * (4 * LB + 1), LANES), F32),
         ],
         compiler_params=grant(dates),
     )(frames, ground)
@@ -343,7 +383,7 @@
         ],
         axis=1,
     ).astype(BF16)
-    return rebuilt.reshape(dates, 2 * LB, cells)
+    return rebuilt.reshape(dates, 4 * LB, cells // 2)
 
 
 def dft_tables(length, span):
@@ -354,19 +394,23 @@
 
 
 def patch_kernel(range_table, ahead_table, back_table, mine, out, wide):
-    blocks, _, cells = mine.shape
+    blocks, rows, _ = mine.shape
+    cells = out.shape[3]
     chunks = cells // LANES
 
     def cut(value, j):
         return value[:, j * LANES : (j + 1) * LANES]
 
     for b in range(blocks):
-        rows = mine[b].astype(F32)
-        for j in range(chunks):
-            wide[j, b * 2 * LB : (b + 1) * 2 * LB, :] = cut(rows, j)
+        block = mine[b].astype(F32)
+        for j in range(chunks // 2):
+            wide[j, b * (rows + 1) : b * (rows + 1) + rows, :] = cut(block, j)
 
     def lines_of(c, j):
-        pieces = [wide[j, pl.ds(c * LB + t, blocks, stride=2 * LB), :] for t in range(LB)]
+        side, j = divmod(j, chunks // 2)
+        pieces = [
+            wide[j, pl.ds((c * LB + t) * 2 + side, blocks, stride=rows + 1), :] for t in range(LB)
+        ]
         return jnp.concatenate(pieces, axis=0).astype(BF16)
 
     first = jnp.concatenate(
@@ -399,17 +443,20 @@
     power = real * real + imaginary * imaginary
     total = jnp.sum(power, axis=0, keepdims=True)
     total = jnp.concatenate([cut(total, j) for j in range(chunks)], axis=0)
-    lane = iota(total.shape, 1)
-    shift = 1
-    while shift < PATCH:
-        other = jnp.where(
-            (lane & shift) == 0, pltpu.roll(total, LANES - shift, 1), pltpu.roll(total, shift, 1)
-        )
-        total = total + other
-        shift *= 2
+    pieces = []
+    for _ in range(3):
+        pieces.append(total.astype(BF16))
+        total = total - pieces[-1].astype(F32)
+    bits = PATCH.bit_length() - 1
+    first, second = iota((LANES, LANES), 0), iota((LANES, LANES), 1)
+    ones = lax.shift_right_logical(first, bits) == lax.shift_right_logical(second, bits)
+    ones = jnp.where(ones, 1.0, 0.0).astype(BF16)
+    pieces = jnp.concatenate(pieces, axis=0)
+    pieces = jnp.dot(pieces, ones, preferred_element_type=F32)
+    total = pieces[:chunks] + (pieces[chunks : 2 * chunks] + pieces[2 * chunks :])
     mean = total * (1.0 / (PATCH * PATCH)) + EPSILON
     mean = jnp.concatenate([mean[j : j + 1] for j in range(chunks)], axis=1)
-    ramp = jnp.sqrt(jnp.sqrt(power / mean))
+    ramp = lax.rsqrt(lax.rsqrt(jnp.maximum(power / mean, SMALLEST)))
     weighted = jnp.concatenate([real * ramp, imaginary * ramp], axis=0).astype(BF16)
     back = jnp.dot(back_table[...], weighted, preferred_element_type=F32).astype(BF16)
     back = by_chunk(back[:PATCH], back[PATCH:])
@@ -420,7 +467,7 @@
 
 
 def patch_filter(mine, lines):
-    cells = mine.shape[2]
+    cells = 2 * mine.shape[2]
     blocks = PATCH // LB
     cosine, sine = dft_tables(PATCH, LANES)
     range_table = np.block([[cosine, -sine], [sine, cosine]])
@@ -437,10 +484,10 @@
             pl.BlockSpec((2 * LANES, 2 * LANES), lambda p: (0, 0)),
             pl.BlockSpec((2 * PATCH, 2 * PATCH), lambda p: (0, 0)),
             pl.BlockSpec((2 * PATCH, 2 * PATCH), lambda p: (0, 0)),
-            pl.BlockSpec((blocks, 2 * LB, cells), lambda p: (p, 0, 0)),
+            pl.BlockSpec((blocks, *mine.shape[1:]), lambda p: (p, 0, 0)),
         ],
         out_specs=pl.BlockSpec((1, 2, PATCH, cells), lambda p: (0, 0, p, 0)),
-        scratch_shapes=[pltpu.VMEM((cells // LANES, blocks * 2 * LB, LANES), F32)],
+        scratch_shapes=[pltpu.VMEM((cells // (2 * LANES), blocks * (4 * LB + 1), LANES), F32)],
         compiler_params=grant(lines // LB),
     )(*tables, mine)
 
@@ -455,7 +502,7 @@
     ground = lax.all_to_all(merged, "date", split_axis=0, concat_axis=0, tiled=True)
     windows = viewing_frames.shape[0]
     fits = devices <= 32 and devices % 16 == 0 and windows % 2 == 0 and LANES % windows == 0
-    fits = fits and salvo_records.shape[4] % (2 * LANES) == 0
+    fits = fits and salvo_records.shape[4] % SEGMENT == 0
     rebuilt = (link if fits else link_plain)(ground, viewing_frames)
     mine = lax.all_to_all(rebuilt, "date", split_axis=0, concat_axis=0, tiled=True)
     return patch_filter(mine, LB * devices)

time: 34.9 us -> 33.7 us (0.966)
  Pallas kernels: 6.01 us -> 4.82 us
    pallas_call x1, Pallas kernels: 2.63 us -> 1.67 us  [link(): pl.pallas_call(link_kernel, out_shape=jax.ShapeDtypeStruct((dates, 4 * LB...]
where the time goes in v4:
time: 33.7 us; the launch traced here: 33.5 us
  blocking collectives  27.9 us (83%)
  Pallas kernels  4.82 us (14%)
  between operations  0.7 us (2%)
    all_to_all x1, blocking collectives, on_device(): lax.all_to_all(merged, 'date', split_axis=0, concat_axis=0, tiled=True)  17.2 us
    all_to_all x1, blocking collectives, on_device(): lax.all_to_all(rebuilt, 'date', split_axis=0, concat_axis=0, tiled=True)  10.7 us
    pallas_call x1, Pallas kernels, link(): pl.pallas_call(link_kernel, out_shape=jax.ShapeDtypeStruct((dates, 4 * LB...  1.67 us
    pallas_call x1, Pallas kernels, seam(): pl.pallas_call(functools.partial(seam_kernel, sweep_labels=LB * devices),...  1.66 us
    pallas_call x1, Pallas kernels, patch_filter(): pl.pallas_call(patch_kernel, grid=(lines // PATCH,), out_shape=jax.ShapeD...  1.49 us

profile of v4, /device:TPU:0, one launch (start us, length us, event | category | flops | bytes accessed | tf_op | source)
XLA Modules:
  0.0 33.5 jit_solution(12571595516038185526)
XLA Ops:
  0.7 1.7 %shard_map.91 = bf16[16,8,1024]{2,1,0:T(8,128)(2,1)S(1)} custom-call(s32[1]{0:T(128)S(6)} %copy.10.refs_0_, s32[1,3]{1,0:T(1,128)} %refs_1_.1, s32[1,2]{1,0:T(1,128)} %refs_2_.1, bf16[1,3,8]{2,1,0:T(4,128)(2,1)} %refs_3_.1, bf16[1,3,13,2,1024]{4,3,2,1,0:T(2,128)(2,1)} %bitcast.1), custom_call_target="tpu_custom_call" | custom-call | tf_op jit(solution)/shard_map/pallas_call | solution.py:118
  2.3 0.0 copy-start.3
  2.3 17.2 %all_to_all.10.ground = bf16[16,8,1024]{2,1,0:T(8,128)(2,1)S(1)} all-to-all(bf16[16,8,1024]{2,1,0:T(8,128)(2,1)S(1)} %shard_map.91), channel_id=1, replica_groups=mesh['group'=2,'date'=16] {'date'}, dimensions={0} | all-to-all | bytes 524288 | tf_op jit(solution)/shard_map/all_to_all | solution.py:502
  19.6 0.0 copy-done.3
  19.6 1.7 %shard_map.92 = bf16[16,8,512]{2,1,0:T(8,128)(2,1)S(1)} custom-call(s32[16,128]{1,0:T(8,128)S(1)} %copy-done.3, bf16[16,8,1024]{2,1,0:T(8,128)(2,1)S(1)} %all_to_all.10.ground), custom_call_target="tpu_custom_call" | custom-call | tf_op jit(solution)/shard_map/pallas_call | solution.py:298
  21.2 0.0 copy-start
  21.2 0.0 copy-start.1
  21.3 0.0 copy-start.2
  21.3 10.7 %all_to_all.11.mine = bf16[16,8,512]{2,1,0:T(8,128)(2,1)S(1)} all-to-all(bf16[16,8,512]{2,1,0:T(8,128)(2,1)S(1)} %shard_map.92), channel_id=1, replica_groups=mesh['group'=2,'date'=16] {'date'}, dimensions={0} | all-to-all | bytes 262144 | tf_op jit(solution)/shard_map/all_to_all | solution.py:507
  32.0 0.0 copy-done
  32.0 0.0 copy-done.1
  32.0 0.0 copy-done.2
  32.0 1.5 %shard_map.93 = bf16[1,2,32,1024]{3,2,1,0:T(8,128)(2,1)} custom-call(bf16[256,256]{1,0:T(8,128)(2,1)S(1)} %copy-done, bf16[64,64]{1,0:T(8,128)(2,1)S(1)} %copy-done.2, bf16[64,64]{1,0:T(8,128)(2,1)S(1)} %copy-done.1, bf16[16,8,512]{2,1,0:T(8,128)(2,1)S(1)} %all_to_all.11.mine), custom_call_target="tpu_custom_call" | custom-call | tf_op jit(solution)/shard_map/pallas_call | solution.py:479
Async XLA Ops:
  2.3 17.2 %copy-start.3 = (s32[16,128]{1,0:T(8,128)S(1)}, s32[16,128]{1,0:T(8,128)}, u32[]{:S(2)}) copy-start(s32[16,128]{1,0:T(8,128)} %frames.1) | copy-start | bytes 24580
  21.2 10.8 %copy-start = (bf16[256,256]{1,0:T(8,128)(2,1)S(1)}, bf16[256,256]{1,0:T(8,128)(2,1)}, u32[]{:S(2)}) copy-start(bf16[256,256]{1,0:T(8,128)(2,1)} %constant.15.range_table) | copy-start | bytes 393220
  21.2 10.7 %copy-start.1 = (bf16[64,64]{1,0:T(8,128)(2,1)S(1)}, bf16[64,64]{1,0:T(8,128)(2,1)}, u32[]{:S(2)}) copy-start(bf16[64,64]{1,0:T(8,128)(2,1)} %constant.17.back_table) | copy-start | bytes 24580
  21.3 10.7 %copy-start.2 = (bf16[64,64]{1,0:T(8,128)(2,1)S(1)}, bf16[64,64]{1,0:T(8,128)(2,1)}, u32[]{:S(2)}) copy-start(bf16[64,64]{1,0:T(8,128)(2,1)} %constant.16.ahead_table) | copy-start | bytes 24580

commit v5 on v4

--- a/solution.py
+++ b/solution.py
@@ -37,17 +37,11 @@
     return pltpu.CompilerParams(vmem_limit_bytes=min(devices, 120) * 2**19)
 
 
-def seam_kernel(*refs, sweep_labels):
-    prior, sources, out = refs[0], refs[1:5], refs[5]
-    (drifts, seams, weights, bursts), (wide, done) = refs[6:10], refs[10:]
-    copies = [
-        pltpu.make_async_copy(source, target, done.at[n])
-        for n, (source, target) in enumerate(zip(sources, refs[6:10]))
-    ]
-    for copy in copies:
-        copy.start()
-    for copy in copies:
-        copy.wait()
+def early_kernel(out):
+    out[...] = jnp.zeros(out.shape, F32)
+
+
+def seam_kernel(prior, bursts, early, drifts, seams, weights, out, wide, *, sweep_labels):
     sweeps, _, cells = bursts.shape[2:]
     slot = wide.shape[0] // SALVO_TALLY
     span = cells + LANES
@@ -63,7 +57,7 @@
     row, column = iota((LANES, LANES), 0), iota((LANES, LANES), 1)
     resampled = []
     for b in range(SALVO_TALLY):
-        first = span + (STENCIL_WEIGHTS // 2 - 1) - drifts[0, b]
+        first = span + (STENCIL_WEIGHTS // 2 - 1) - jnp.max(drifts[0:1, b : b + 1])
         first = jnp.where(first >= span, first - span, first)
         rotated = jnp.concatenate(
             [wide[b * slot : (b + 1) * slot, :], jnp.zeros((slot, LANES), F32)], axis=1
@@ -95,11 +89,11 @@
     for b in range(SALVO_TALLY):
         ramp = jnp.ones(shape, F32)
         if b > 0:
-            start = start + sweeps - seams[0, b - 1]
-            up = (line - start + 1).astype(F32) / (seams[0, b - 1] + 1).astype(F32)
+            start = start + sweeps - seams[0:1, b - 1 : b]
+            up = (line - start + 1).astype(F32) / (seams[0:1, b - 1 : b] + 1).astype(F32)
             ramp = ramp * jnp.clip(up, 0.0, 1.0)
         if b < SALVO_TALLY - 1:
-            down = (start + sweeps - line).astype(F32) / (seams[0, b] + 1).astype(F32)
+            down = (start + sweeps - line).astype(F32) / (seams[0:1, b : b + 1] + 1).astype(F32)
             ramp = ramp * jnp.clip(down, 0.0, 1.0)
         place = jnp.where((which == b) & (line == start + entry), ramp, place)
     inside = (entry < sweeps) & (column & 1 == part) & (line >= 0) & (line < sweep_labels)
@@ -114,25 +108,25 @@
     while slot < 2 * sweeps:
         slot *= 2
     bursts = bursts.transpose(0, 1, 3, 2, 4)
-    arrays = (drifts, seams, weights, bursts)
+    early = pl.pallas_call(
+        early_kernel,
+        out_shape=jax.ShapeDtypeStruct((8, LANES), F32),
+        compiler_params=grant(devices),
+        cost_estimate=pl.CostEstimate(flops=10**8, bytes_accessed=4096, transcendentals=0),
+    )()
     return pl.pallas_call(
         functools.partial(seam_kernel, sweep_labels=LB * devices),
         out_shape=jax.ShapeDtypeStruct((devices, 2 * HALO, cells), BF16),
         in_specs=[
             pl.BlockSpec(memory_space=pltpu.SMEM),
-            *[pl.BlockSpec(memory_space=pltpu.HBM)] * len(arrays),
+            *[pl.BlockSpec(memory_space=pltpu.VMEM)] * 5,
         ],
         out_specs=pl.BlockSpec(memory_space=pltpu.VMEM),
         scratch_shapes=[
-            pltpu.SMEM(drifts.shape, jnp.int32),
-            pltpu.SMEM(seams.shape, jnp.int32),
-            pltpu.VMEM(weights.shape, BF16),
-            pltpu.VMEM(bursts.shape, BF16),
             pltpu.VMEM((SALVO_TALLY * slot, cells), F32),
-            pltpu.SemaphoreType.DMA((len(arrays),)),
         ],
         compiler_params=grant(devices),
-    )(prior, *[pltpu.with_memory_space_constraint(x, pltpu.HBM) for x in arrays])
+    )(prior, bursts, early, drifts, seams, weights)
 
 
 def link_kernel(frames, ground, out, wide, right32, gam, rebuilt):

time: 33.7 us -> 33.5 us (level)
  Pallas kernels: 4.82 us -> 3.84 us
  local copies, waits for them, and re-layouts: 0.03 us -> 0.72 us
    pallas_call x1, Pallas kernels: 1.66 us -> 0.67 us  [seam(): pl.pallas_call(functools.partial(seam_kernel, sweep_labels=LB * devices),...]
    unnamed x8 -> x16, local copies, waits for them, and re-layouts: 0.03 us -> 0.72 us
where the time goes in v5:
time: 33.5 us; the launch traced here: 33.2 us
  blocking collectives  27.9 us (83%)
  Pallas kernels  3.84 us (11%)
  between operations  0.75 us (2%)
  local copies, waits for them, and re-layouts  0.72 us (2%)
    all_to_all x1, blocking collectives, on_device(): lax.all_to_all(merged, 'date', split_axis=0, concat_axis=0, tiled=True)  17.2 us
    all_to_all x1, blocking collectives, on_device(): lax.all_to_all(rebuilt, 'date', split_axis=0, concat_axis=0, tiled=True)  10.7 us
    pallas_call x1, Pallas kernels, link(): pl.pallas_call(link_kernel, out_shape=jax.ShapeDtypeStruct((dates, 4 * LB...  1.68 us
    pallas_call x1, Pallas kernels, patch_filter(): pl.pallas_call(patch_kernel, grid=(lines // PATCH,), out_shape=jax.ShapeD...  1.49 us
    unnamed x16, local copies, waits for them, and re-layouts  0.72 us

profile of v5, /device:TPU:0, one launch (start us, length us, event | category | flops | bytes accessed | tf_op | source)
XLA Modules:
  0.0 33.2 jit_solution(18297056943211143863)
XLA Ops:
  0.0 0.0 copy-start
  0.0 0.0 copy-start.7
  0.7 0.0 copy-start.5
  0.7 0.0 copy-start.6
  0.7 0.2 copy-done
  0.9 0.0 copy-done.7
  0.9 0.5 %copy-done.5 = bf16[1,3,8]{2,1,0:T(4,128)(2,1)S(1)} copy-done((bf16[1,3,8]{2,1,0:T(4,128)(2,1)S(1)}, bf16[1,3,8]{2,1,0:T(4,128)(2,1)}, u32[]{:S(2)}) %copy-start.5) | copy-done | bytes 72
  1.4 0.0 copy-done.6
  1.4 0.7 %shard_map.92 = bf16[16,8,1024]{2,1,0:T(8,128)(2,1)S(1)} custom-call(s32[1]{0:T(128)S(6)} %copy.10.prior, bf16[1,3,13,2,1024]{4,3,2,1,0:T(2,128)(2,1)S(1)} %bitcast.1, f32[8,128]{1,0:T(8,128)S(1)} %shard_map.91.early, s32[1,3]{1,0:T(1,128)S(1)} %copy-done.6, s32[1,2]{1,0:T(1,128)S(1)} %copy-done.7, bf16[1,3,8]{2,1,0:T(4,128)(2,1)S(1)} %copy-done.5), custom_call_target="tpu_custom_call" | custom-call | tf_op jit(solution)/shard_map/pallas_call | solution.py:117
  2.1 0.0 copy-start.4
  2.1 17.2 %all_to_all.10.ground = bf16[16,8,1024]{2,1,0:T(8,128)(2,1)S(1)} all-to-all(bf16[16,8,1024]{2,1,0:T(8,128)(2,1)S(1)} %shard_map.92), channel_id=1, replica_groups=mesh['group'=2,'date'=16] {'date'}, dimensions={0} | all-to-all | bytes 524288 | tf_op jit(solution)/shard_map/all_to_all | solution.py:496
  19.3 0.0 copy-done.4
  19.3 1.7 %shard_map.93 = bf16[16,8,512]{2,1,0:T(8,128)(2,1)S(1)} custom-call(s32[16,128]{1,0:T(8,128)S(1)} %copy-done.4, bf16[16,8,1024]{2,1,0:T(8,128)(2,1)S(1)} %all_to_all.10.ground), custom_call_target="tpu_custom_call" | custom-call | tf_op jit(solution)/shard_map/pallas_call | solution.py:292
  21.0 0.0 copy-start.1
  21.0 0.0 copy-start.2
  21.0 0.0 copy-start.3
  21.0 10.7 %all_to_all.11.mine = bf16[16,8,512]{2,1,0:T(8,128)(2,1)S(1)} all-to-all(bf16[16,8,512]{2,1,0:T(8,128)(2,1)S(1)} %shard_map.93), channel_id=1, replica_groups=mesh['group'=2,'date'=16] {'date'}, dimensions={0} | all-to-all | bytes 262144 | tf_op jit(solution)/shard_map/all_to_all | solution.py:501
  31.7 0.0 copy-done.1
  31.7 0.0 copy-done.2
  31.7 0.0 copy-done.3
  31.7 1.5 %shard_map.94 = bf16[1,2,32,1024]{3,2,1,0:T(8,128)(2,1)} custom-call(bf16[256,256]{1,0:T(8,128)(2,1)S(1)} %copy-done.1, bf16[64,64]{1,0:T(8,128)(2,1)S(1)} %copy-done.3, bf16[64,64]{1,0:T(8,128)(2,1)S(1)} %copy-done.2, bf16[16,8,512]{2,1,0:T(8,128)(2,1)S(1)} %all_to_all.11.mine), custom_call_target="tpu_custom_call" | custom-call | tf_op jit(solution)/shard_map/pallas_call | solution.py:473
  (1 shorter events, 0.0 us)
Async XLA Ops:
  0.0 0.9 %copy-start = (bf16[1,3,2,13,1024]{4,2,3,1,0:T(2,128)(2,1)S(1)}, bf16[1,3,2,13,1024]{4,2,3,1,0:T(2,128)(2,1)}, u32[]{:S(2)}) copy-start(bf16[1,3,2,13,1024]{4,2,3,1,0:T(2,128)(2,1)} %param.9) | copy-start | bytes 479236
  0.0 0.9 %copy-start.7 = (s32[1,2]{1,0:T(1,128)S(1)}, s32[1,2]{1,0:T(1,128)}, u32[]{:S(2)}) copy-start(s32[1,2]{1,0:T(1,128)} %seams.1) | copy-start | bytes 28
  0.7 0.7 %copy-start.5 = (bf16[1,3,8]{2,1,0:T(4,128)(2,1)S(1)}, bf16[1,3,8]{2,1,0:T(4,128)(2,1)}, u32[]{:S(2)}) copy-start(bf16[1,3,8]{2,1,0:T(4,128)(2,1)} %weights.1) | copy-start | bytes 148
  0.7 0.7 %copy-start.6 = (s32[1,3]{1,0:T(1,128)S(1)}, s32[1,3]{1,0:T(1,128)}, u32[]{:S(2)}) copy-start(s32[1,3]{1,0:T(1,128)} %drifts.1) | copy-start | bytes 40
  2.1 17.2 %copy-start.4 = (s32[16,128]{1,0:T(8,128)S(1)}, s32[16,128]{1,0:T(8,128)}, u32[]{:S(2)}) copy-start(s32[16,128]{1,0:T(8,128)} %frames.1) | copy-start | bytes 24580
  21.0 10.7 %copy-start.1 = (bf16[256,256]{1,0:T(8,128)(2,1)S(1)}, bf16[256,256]{1,0:T(8,128)(2,1)}, u32[]{:S(2)}) copy-start(bf16[256,256]{1,0:T(8,128)(2,1)} %constant.15.range_table) | copy-start | bytes 393220
  21.0 10.7 %copy-start.2 = (bf16[64,64]{1,0:T(8,128)(2,1)S(1)}, bf16[64,64]{1,0:T(8,128)(2,1)}, u32[]{:S(2)}) copy-start(bf16[64,64]{1,0:T(8,128)(2,1)} %constant.17.back_table) | copy-start | bytes 24580
  21.0 10.7 %copy-start.3 = (bf16[64,64]{1,0:T(8,128)(2,1)S(1)}, bf16[64,64]{1,0:T(8,128)(2,1)}, u32[]{:S(2)}) copy-start(bf16[64,64]{1,0:T(8,128)(2,1)} %constant.16.ahead_table) | copy-start | bytes 24580

commit v6 on v5

--- a/solution.py
+++ b/solution.py
@@ -16,7 +16,7 @@
 ITERS = 8
 PATCH = 32
 LANES = 128
-SEGMENT = 512
+SEGMENT = 256
 BATCH = 8
 
 EPSILON = 1e-06
@@ -449,9 +449,11 @@
     pieces = jnp.dot(pieces, ones, preferred_element_type=F32)
     total = pieces[:chunks] + (pieces[chunks : 2 * chunks] + pieces[2 * chunks :])
     mean = total * (1.0 / (PATCH * PATCH)) + EPSILON
-    mean = jnp.concatenate([mean[j : j + 1] for j in range(chunks)], axis=1)
-    ramp = lax.rsqrt(lax.rsqrt(jnp.maximum(power / mean, SMALLEST)))
-    weighted = jnp.concatenate([real * ramp, imaginary * ramp], axis=0).astype(BF16)
+    level = jnp.sqrt(lax.rsqrt(mean))
+    level = jnp.concatenate([level[j : j + 1] for j in range(chunks)], axis=1)
+    ramp = lax.rsqrt(lax.rsqrt(jnp.maximum(power, SMALLEST)))
+    weighted = jnp.concatenate([real * ramp * level, imaginary * ramp * level], axis=0)
+    weighted = weighted.astype(BF16)
     back = jnp.dot(back_table[...], weighted, preferred_element_type=F32).astype(BF16)
     back = by_chunk(back[:PATCH], back[PATCH:])
     final = lax.dot_general(back, table, NT, preferred_element_type=F32)

time: 33.5 us -> 33.5 us (level)
  no operation moved by 1% of the time
where the time goes in v6:
time: 33.5 us; the launch traced here: 33.2 us
  blocking collectives  27.9 us (83%)
  Pallas kernels  3.8 us (11%)
  between operations  0.75 us (2%)
  local copies, waits for them, and re-layouts  0.72 us (2%)
    all_to_all x1, blocking collectives, on_device(): lax.all_to_all(merged, 'date', split_axis=0, concat_axis=0, tiled=True)  17.2 us
    all_to_all x1, blocking collectives, on_device(): lax.all_to_all(rebuilt, 'date', split_axis=0, concat_axis=0, tiled=True)  10.7 us
    pallas_call x1, Pallas kernels, link(): pl.pallas_call(link_kernel, out_shape=jax.ShapeDtypeStruct((dates, 4 * LB...  1.66 us
    pallas_call x1, Pallas kernels, patch_filter(): pl.pallas_call(patch_kernel, grid=(lines // PATCH,), out_shape=jax.ShapeD...  1.47 us
    unnamed x16, local copies, waits for them, and re-layouts  0.72 us

profile of v6, /device:TPU:0, one launch (start us, length us, event | category | flops | bytes accessed | tf_op | source)
XLA Modules:
  0.0 33.2 jit_solution(16537385758722493249)
XLA Ops:
  0.0 0.0 copy-start
  0.0 0.0 copy-start.7
  0.7 0.0 copy-start.5
  0.7 0.0 copy-start.6
  0.7 0.2 copy-done
  0.9 0.0 copy-done.7
  0.9 0.5 %copy-done.5 = bf16[1,3,8]{2,1,0:T(4,128)(2,1)S(1)} copy-done((bf16[1,3,8]{2,1,0:T(4,128)(2,1)S(1)}, bf16[1,3,8]{2,1,0:T(4,128)(2,1)}, u32[]{:S(2)}) %copy-start.5) | copy-done | bytes 72
  1.4 0.0 copy-done.6
  1.4 0.7 %shard_map.92 = bf16[16,8,1024]{2,1,0:T(8,128)(2,1)S(1)} custom-call(s32[1]{0:T(128)S(6)} %copy.10.prior, bf16[1,3,13,2,1024]{4,3,2,1,0:T(2,128)(2,1)S(1)} %bitcast.1, f32[8,128]{1,0:T(8,128)S(1)} %shard_map.91.early, s32[1,3]{1,0:T(1,128)S(1)} %copy-done.6, s32[1,2]{1,0:T(1,128)S(1)} %copy-done.7, bf16[1,3,8]{2,1,0:T(4,128)(2,1)S(1)} %copy-done.5), custom_call_target="tpu_custom_call" | custom-call | tf_op jit(solution)/shard_map/pallas_call | solution.py:117
  2.1 0.0 copy-start.4
  2.1 17.2 %all_to_all.10.ground = bf16[16,8,1024]{2,1,0:T(8,128)(2,1)S(1)} all-to-all(bf16[16,8,1024]{2,1,0:T(8,128)(2,1)S(1)} %shard_map.92), channel_id=1, replica_groups=mesh['group'=2,'date'=16] {'date'}, dimensions={0} | all-to-all | bytes 524288 | tf_op jit(solution)/shard_map/all_to_all | solution.py:498
  19.3 0.0 copy-done.4
  19.3 1.7 %shard_map.93 = bf16[16,8,512]{2,1,0:T(8,128)(2,1)S(1)} custom-call(s32[16,128]{1,0:T(8,128)S(1)} %copy-done.4, bf16[16,8,1024]{2,1,0:T(8,128)(2,1)S(1)} %all_to_all.10.ground), custom_call_target="tpu_custom_call" | custom-call | tf_op jit(solution)/shard_map/pallas_call | solution.py:292
  21.0 0.0 copy-start.1
  21.0 0.0 copy-start.2
  21.0 0.0 copy-start.3
  21.0 10.7 %all_to_all.11.mine = bf16[16,8,512]{2,1,0:T(8,128)(2,1)S(1)} all-to-all(bf16[16,8,512]{2,1,0:T(8,128)(2,1)S(1)} %shard_map.93), channel_id=1, replica_groups=mesh['group'=2,'date'=16] {'date'}, dimensions={0} | all-to-all | bytes 262144 | tf_op jit(solution)/shard_map/all_to_all | solution.py:503
  31.7 0.0 copy-done.1
  31.7 0.0 copy-done.2
  31.7 0.0 copy-done.3
  31.7 1.5 %shard_map.94 = bf16[1,2,32,1024]{3,2,1,0:T(8,128)(2,1)} custom-call(bf16[256,256]{1,0:T(8,128)(2,1)S(1)} %copy-done.1, bf16[64,64]{1,0:T(8,128)(2,1)S(1)} %copy-done.3, bf16[64,64]{1,0:T(8,128)(2,1)S(1)} %copy-done.2, bf16[16,8,512]{2,1,0:T(8,128)(2,1)S(1)} %all_to_all.11.mine), custom_call_target="tpu_custom_call" | custom-call | tf_op jit(solution)/shard_map/pallas_call | solution.py:475
  (1 shorter events, 0.0 us)
Async XLA Ops:
  0.0 0.9 %copy-start = (bf16[1,3,2,13,1024]{4,2,3,1,0:T(2,128)(2,1)S(1)}, bf16[1,3,2,13,1024]{4,2,3,1,0:T(2,128)(2,1)}, u32[]{:S(2)}) copy-start(bf16[1,3,2,13,1024]{4,2,3,1,0:T(2,128)(2,1)} %param.9) | copy-start | bytes 479236
  0.0 0.9 %copy-start.7 = (s32[1,2]{1,0:T(1,128)S(1)}, s32[1,2]{1,0:T(1,128)}, u32[]{:S(2)}) copy-start(s32[1,2]{1,0:T(1,128)} %seams.1) | copy-start | bytes 28
  0.7 0.7 %copy-start.5 = (bf16[1,3,8]{2,1,0:T(4,128)(2,1)S(1)}, bf16[1,3,8]{2,1,0:T(4,128)(2,1)}, u32[]{:S(2)}) copy-start(bf16[1,3,8]{2,1,0:T(4,128)(2,1)} %weights.1) | copy-start | bytes 148
  0.7 0.7 %copy-start.6 = (s32[1,3]{1,0:T(1,128)S(1)}, s32[1,3]{1,0:T(1,128)}, u32[]{:S(2)}) copy-start(s32[1,3]{1,0:T(1,128)} %drifts.1) | copy-start | bytes 40
  2.1 17.2 %copy-start.4 = (s32[16,128]{1,0:T(8,128)S(1)}, s32[16,128]{1,0:T(8,128)}, u32[]{:S(2)}) copy-start(s32[16,128]{1,0:T(8,128)} %frames.1) | copy-start | bytes 24580
  21.0 10.8 %copy-start.1 = (bf16[256,256]{1,0:T(8,128)(2,1)S(1)}, bf16[256,256]{1,0:T(8,128)(2,1)}, u32[]{:S(2)}) copy-start(bf16[256,256]{1,0:T(8,128)(2,1)} %constant.15.range_table) | copy-start | bytes 393220
  21.0 10.7 %copy-start.2 = (bf16[64,64]{1,0:T(8,128)(2,1)S(1)}, bf16[64,64]{1,0:T(8,128)(2,1)}, u32[]{:S(2)}) copy-start(bf16[64,64]{1,0:T(8,128)(2,1)} %constant.17.back_table) | copy-start | bytes 24580
  21.0 10.7 %copy-start.3 = (bf16[64,64]{1,0:T(8,128)(2,1)S(1)}, bf16[64,64]{1,0:T(8,128)(2,1)}, u32[]{:S(2)}) copy-start(bf16[64,64]{1,0:T(8,128)(2,1)} %constant.16.ahead_table) | copy-start | bytes 24580
